TPU v7x, 32 devices: a whole 2x2x4 slice. The times are simulated.
32 devices in a mesh: seq: 8 (over y, x, core), wshard: 4 (over z).
Axes of the slice: x: 2, y: 2, z: 4, core: 2. Of those that a mesh axis runs over, the one named last changes fastest.
Arguments:
- tokens: float32 [6144, 768], P(('seq', 'wshard')), may hold values from -18 to 18, as said below
- attention_norm_gain: float32 [2, 768], replicated, may hold values from 0.5 to 1.5
- qkv_weight: bfloat16 [2, 768, 2304], P(None, None, 'wshard'), may hold values from -7 to 7, as said below
- output_weight: bfloat16 [2, 768, 768], P(None, None, 'wshard'), may hold values from -0.75 to 0.75
- feedforward_norm_gain: float32 [2, 768], replicated, may hold values from 0.5 to 1.5
- input_weight: bfloat16 [2, 768, 2304], P(None, None, 'wshard'), may hold values from -0.21875 to 0.21875
- down_weight: bfloat16 [2, 1152, 768], P(None, 'wshard'), may hold values from -0.1875 to 0.1875
- cotangent: float32 [6144, 768], P(('seq', 'wshard')), may hold values from -18 to 18
Outputs:
- outputs: float32 [6144, 768], P(('seq', 'wshard'))
- input_grad: float32 [6144, 768], P(('seq', 'wshard'))
- grad_attention_gain: float32 [2, 768], replicated
- grad_qkv_weight: float32 [2, 768, 2304], P(None, 'seq', 'wshard')
- grad_output_weight: float32 [2, 768, 768], P(None, 'seq', 'wshard')
- grad_feedforward_gain: float32 [2, 768], replicated
- grad_input_weight: float32 [2, 768, 2304], P(None, 'seq', 'wshard')
- grad_down_weight: float32 [2, 1152, 768], P(None, 'wshard', 'seq')
Inputs may be any that keep to these rules, and one draw needn't show every extreme that they name: `tokens`: activations of the first layer. `qkv_weight`: columns hold queries, keys, values, each head by head.
All inputs are finite; a program needn't handle non-finite values.
Results may differ from a plain program's by a relative error of at most 0.022.
Values may be sent and summed in bfloat16 or wider, within the bound.
A program may use at most 192 MiB of HBM per device.

v0:
```python
import math

import jax
import jax.numpy as jnp
from jax import lax
from jax.sharding import PartitionSpec as P

D = 768
HEADS = 12
HDIM = 64
FF = 1152
WIN = 64
LAYERS = 2
SEQS = 1


EPSILON = 1e-05
THETA = 10000.0


def with_halo(cells, sides, width):
    for axis, dim in sides:
        count = lax.axis_size(axis)
        ends = count - 1
        head = lax.slice_in_dim(cells, 0, width, axis=dim)
        tail = lax.slice_in_dim(cells, cells.shape[dim] - width, cells.shape[dim], axis=dim)
        cells = jnp.concatenate(
            [
                lax.ppermute(tail, axis, [(i, (i + 1) % count) for i in range(ends)]),
                cells,
                lax.ppermute(head, axis, [((i + 1) % count, i) for i in range(ends)]),
            ],
            axis=dim,
        )
    return cells


def rotate_half(values):
    middle_state = values.shape[-1] // 2
    return jnp.concatenate([-values[..., middle_state:], values[..., :middle_state]], axis=-1)


def rope_tables(positions):
    middle_state = HDIM // 2
    inverse = THETA ** (-(jnp.arange(middle_state, dtype=jnp.float32) * (2.0 / HDIM)))
    angles = positions.astype(jnp.float32)[:, None] * inverse[None, :]
    cosine = jnp.concatenate([jnp.cos(angles), jnp.cos(angles)], axis=1)
    sine = jnp.concatenate([jnp.sin(angles), jnp.sin(angles)], axis=1)
    return (cosine[:, None, :], sine[:, None, :])


def apply_rope(values, cosine, sine):
    return values * cosine + rotate_half(values) * sine


def undo_rope(grads, cosine, sine):
    return grads * cosine - rotate_half(grads * sine)


def layer_normalize(hidden_state):
    centred = hidden_state - jnp.mean(hidden_state, axis=-1, keepdims=True)
    inverse = lax.rsqrt(jnp.mean(centred * centred, axis=-1, keepdims=True) + EPSILON)
    return (centred * inverse, inverse)


def norm_backward_step(normalized_gradient, normed, inverse, gain_row):
    scaled = normalized_gradient * gain_row
    result = (
        scaled
        - jnp.mean(scaled, axis=-1, keepdims=True)
        - normed * jnp.mean(scaled * normed, axis=-1, keepdims=True)
    )
    return (result * inverse, jnp.sum(normalized_gradient * normed, axis=0))


def gelu_exact(inner_activation):
    return 0.5 * inner_activation * (1.0 + lax.erf(inner_activation * (1.0 / math.sqrt(2.0))))


def gelu_slope(inner_activation):
    return 0.5 * (
        1.0 + lax.erf(inner_activation * (1.0 / math.sqrt(2.0)))
    ) + inner_activation * jnp.exp(-0.5 * inner_activation * inner_activation) * (
        1.0 / math.sqrt(2.0 * math.pi)
    )


def band_mask(query_pos, key_pos, length):
    near = jnp.abs(query_pos[:, None] - key_pos[None, :]) <= WIN
    same = query_pos[:, None] // length == key_pos[None, :] // length
    return near & same


def masked_scores(query_matrix, padded_keys, allowed):
    scores = jnp.einsum(
        "qhd,khd->hqk", query_matrix, padded_keys, preferred_element_type=jnp.float32
    ) * (1.0 / math.sqrt(HDIM))
    return jnp.where(allowed[None], scores, -1e30)


def attend_forward(query_matrix, padded_keys, padded_values, allowed):
    scores = masked_scores(query_matrix, padded_keys, allowed)
    top = jnp.max(scores, axis=-1, keepdims=True)
    log_total = top + jnp.log(jnp.sum(jnp.exp(scores - top), axis=-1, keepdims=True))
    probs = jnp.exp(scores - log_total).astype(jnp.bfloat16)
    context_rows = jnp.einsum(
        "hqk,khd->qhd", probs, padded_values, preferred_element_type=jnp.float32
    ).astype(jnp.bfloat16)
    return (context_rows, log_total)


def attend_backward(query_matrix, padded_keys, padded_values, allowed, log_total, grad_context):
    scores = masked_scores(query_matrix, padded_keys, allowed)
    probs = jnp.exp(scores - log_total)
    grad_values = jnp.einsum(
        "hqk,qhd->khd", probs.astype(jnp.bfloat16), grad_context, preferred_element_type=jnp.float32
    )
    grad_probs = jnp.einsum(
        "qhd,khd->hqk", grad_context, padded_values, preferred_element_type=jnp.float32
    )
    grad_scores = (
        probs
        * (grad_probs - jnp.sum(probs * grad_probs, axis=-1, keepdims=True))
        * (1.0 / math.sqrt(HDIM))
    ).astype(jnp.bfloat16)
    grad_queries = jnp.einsum(
        "hqk,khd->qhd", grad_scores, padded_keys, preferred_element_type=jnp.float32
    )
    grad_keys = jnp.einsum(
        "hqk,qhd->khd", grad_scores, query_matrix, preferred_element_type=jnp.float32
    )
    return (grad_queries, grad_keys, grad_values)


def per_device(
    tokens,
    attention_norm_gain,
    qkv_weight,
    output_weight,
    feedforward_norm_gain,
    input_weight,
    down_weight,
    cotangent,
):
    rows = tokens.shape[0]
    total_tokens = rows * lax.axis_size("seq") * lax.axis_size("wshard")
    length = total_tokens // SEQS
    block_index = lax.axis_index("seq") * lax.axis_size("wshard") + lax.axis_index("wshard")
    query_pos = block_index * rows + jnp.arange(rows, dtype=jnp.int32)
    key_pos = block_index * rows - WIN + jnp.arange(rows + 2 * WIN, dtype=jnp.int32)
    allowed = band_mask(query_pos, key_pos, length)
    cosine, sine = rope_tables(query_pos % length)
    scale_grad = 1.0 / math.sqrt(total_tokens)
    hidden_state = tokens
    saved_activations = []
    for layer_number in range(LAYERS):
        gathered = (
            lax.all_gather(qkv_weight[layer_number], "wshard", axis=1, tiled=True),
            lax.all_gather(output_weight[layer_number], "wshard", axis=1, tiled=True),
            lax.all_gather(input_weight[layer_number], "wshard", axis=1, tiled=True),
            lax.all_gather(down_weight[layer_number], "wshard", axis=0, tiled=True),
        )
        full_qkv, full_out, full_in, full_down = gathered
        attention_standardized, attention_inverse_deviation = layer_normalize(hidden_state)
        attention_normalized = (attention_standardized * attention_norm_gain[layer_number]).astype(
            jnp.bfloat16
        )
        qkv = jnp.dot(attention_normalized, full_qkv, preferred_element_type=jnp.float32)
        query_matrix = apply_rope(qkv[:, :D].reshape(rows, HEADS, HDIM), cosine, sine).astype(
            jnp.bfloat16
        )
        key_rows = (
            apply_rope(qkv[:, D : 2 * D].reshape(rows, HEADS, HDIM), cosine, sine)
            .astype(jnp.bfloat16)
            .reshape(rows, D)
        )
        value_rows = qkv[:, 2 * D :].astype(jnp.bfloat16)
        edged = with_halo(
            jnp.concatenate([key_rows, value_rows], axis=1), ((("seq", "wshard"), 0),), WIN
        )
        padded_keys = edged[:, :D].reshape(rows + 2 * WIN, HEADS, HDIM)
        padded_values = edged[:, D:].reshape(rows + 2 * WIN, HEADS, HDIM)
        context_rows, log_total = attend_forward(query_matrix, padded_keys, padded_values, allowed)
        context_rows = context_rows.reshape(rows, D)
        middle_state = hidden_state + jnp.dot(
            context_rows, full_out, preferred_element_type=jnp.float32
        )
        feedforward_standardized, feedforward_inverse_deviation = layer_normalize(middle_state)
        feedforward_normalized = (
            feedforward_standardized * feedforward_norm_gain[layer_number]
        ).astype(jnp.bfloat16)
        inner_activation = jnp.dot(
            feedforward_normalized, full_in, preferred_element_type=jnp.float32
        )
        gated_linear_output = (
            gelu_exact(inner_activation[:, :FF]) * inner_activation[:, FF:]
        ).astype(jnp.bfloat16)
        holding = None
        saved_activations.append(
            (
                holding,
                attention_standardized,
                attention_inverse_deviation,
                attention_normalized,
                query_matrix,
                padded_keys,
                padded_values,
                log_total,
                context_rows,
                feedforward_standardized,
                feedforward_inverse_deviation,
                feedforward_normalized,
                inner_activation,
                gated_linear_output,
            )
        )
        hidden_state = middle_state + jnp.dot(
            gated_linear_output, full_down, preferred_element_type=jnp.float32
        )
    grad = cotangent
    list_again, list_qkv, list_out, list_fgain, list_in, list_down = ([], [], [], [], [], [])
    for layer_number in reversed(range(LAYERS)):
        (
            holding,
            attention_standardized,
            attention_inverse_deviation,
            attention_normalized,
            query_matrix,
            padded_keys,
            padded_values,
            log_total,
            context_rows,
            feedforward_standardized,
            feedforward_inverse_deviation,
            feedforward_normalized,
            inner_activation,
            gated_linear_output,
        ) = saved_activations[layer_number]
        full_qkv, full_out, full_in, full_down = (
            lax.all_gather(qkv_weight[layer_number], "wshard", axis=1, tiled=True),
            lax.all_gather(output_weight[layer_number], "wshard", axis=1, tiled=True),
            lax.all_gather(input_weight[layer_number], "wshard", axis=1, tiled=True),
            lax.all_gather(down_weight[layer_number], "wshard", axis=0, tiled=True),
        )
        grad_rounded = grad.astype(jnp.bfloat16)
        local_down = (
            jnp.dot(gated_linear_output.T, grad_rounded, preferred_element_type=jnp.float32)
            * scale_grad
        )
        grad_geglu = jnp.dot(grad_rounded, full_down.T, preferred_element_type=jnp.float32)
        gate = inner_activation[:, :FF]
        upper = inner_activation[:, FF:]
        grad_inner = jnp.concatenate(
            [grad_geglu * upper * gelu_slope(gate), grad_geglu * gelu_exact(gate)], axis=1
        ).astype(jnp.bfloat16)
        local_in = (
            jnp.dot(feedforward_normalized.T, grad_inner, preferred_element_type=jnp.float32)
            * scale_grad
        )
        normalized_gradient = jnp.dot(grad_inner, full_in.T, preferred_element_type=jnp.float32)
        partial_gradient, feedforward_gain_gradient = norm_backward_step(
            normalized_gradient,
            feedforward_standardized,
            feedforward_inverse_deviation,
            feedforward_norm_gain[layer_number],
        )
        list_fgain.append(feedforward_gain_gradient * scale_grad)
        grad_middle = grad + partial_gradient
        grad_middle_rounded = grad_middle.astype(jnp.bfloat16)
        local_out = (
            jnp.dot(context_rows.T, grad_middle_rounded, preferred_element_type=jnp.float32)
            * scale_grad
        )
        grad_context = (
            jnp.dot(grad_middle_rounded, full_out.T, preferred_element_type=jnp.float32)
            .astype(jnp.bfloat16)
            .reshape(rows, HEADS, HDIM)
        )
        grad_queries, grad_keys, grad_values = attend_backward(
            query_matrix, padded_keys, padded_values, allowed, log_total, grad_context
        )
        edge_terms = jnp.concatenate(
            [grad_keys.reshape(rows + 2 * WIN, D), grad_values.reshape(rows + 2 * WIN, D)], axis=1
        )
        rims = jnp.concatenate([edge_terms[:WIN], edge_terms[rows + WIN :]], axis=0)
        returned = with_halo(rims.astype(jnp.bfloat16), ((("seq", "wshard"), 0),), WIN).astype(
            rims.dtype
        )
        local_terms = edge_terms[WIN : WIN + rows]
        local_terms = (
            local_terms.at[:WIN].add(returned[:WIN]).at[rows - WIN :].add(returned[3 * WIN :])
        )
        grad_keys_local = local_terms[:, :D].reshape(rows, HEADS, HDIM)
        grad_qkv = jnp.concatenate(
            [
                undo_rope(grad_queries, cosine, sine).reshape(rows, D),
                undo_rope(grad_keys_local, cosine, sine).reshape(rows, D),
                local_terms[:, D:],
            ],
            axis=1,
        ).astype(jnp.bfloat16)
        local_qkv = (
            jnp.dot(attention_normalized.T, grad_qkv, preferred_element_type=jnp.float32)
            * scale_grad
        )
        attention_normalized_gradient = jnp.dot(
            grad_qkv, full_qkv.T, preferred_element_type=jnp.float32
        )
        attention_partial_gradient, attention_gain_gradient = norm_backward_step(
            attention_normalized_gradient,
            attention_standardized,
            attention_inverse_deviation,
            attention_norm_gain[layer_number],
        )
        list_again.append(attention_gain_gradient * scale_grad)
        grad = grad_middle + attention_partial_gradient
        partial_sums = (
            lax.psum_scatter(local_qkv, "seq", scatter_dimension=0, tiled=True),
            lax.psum_scatter(local_out, "seq", scatter_dimension=0, tiled=True),
            lax.psum_scatter(local_in, "seq", scatter_dimension=0, tiled=True),
            lax.psum_scatter(local_down, "seq", scatter_dimension=1, tiled=True),
        )
        reduced = (
            lax.psum_scatter(
                partial_sums[0].astype(jnp.bfloat16), "wshard", scatter_dimension=1, tiled=True
            ).astype(jnp.float32),
            lax.psum_scatter(
                partial_sums[1].astype(jnp.bfloat16), "wshard", scatter_dimension=1, tiled=True
            ).astype(jnp.float32),
            lax.psum_scatter(
                partial_sums[2].astype(jnp.bfloat16), "wshard", scatter_dimension=1, tiled=True
            ).astype(jnp.float32),
            lax.psum_scatter(
                partial_sums[3].astype(jnp.bfloat16), "wshard", scatter_dimension=0, tiled=True
            ).astype(jnp.float32),
        )
        list_qkv.append(reduced[0])
        list_out.append(reduced[1])
        list_in.append(reduced[2])
        list_down.append(reduced[3])
    gain_sums = lax.psum(
        (jnp.stack(list_again[::-1]), jnp.stack(list_fgain[::-1])), ("seq", "wshard")
    )
    return (
        hidden_state,
        grad,
        gain_sums[0],
        jnp.stack(list_qkv[::-1]),
        jnp.stack(list_out[::-1]),
        gain_sums[1],
        jnp.stack(list_in[::-1]),
        jnp.stack(list_down[::-1]),
    )


def solution(mesh):
    placed = (
        P(("seq", "wshard"), None),
        P(),
        P(None, None, "wshard"),
        P(None, None, "wshard"),
        P(),
        P(None, None, "wshard"),
        P(None, "wshard", None),
        P(("seq", "wshard"), None),
    )
    return jax.shard_map(
        per_device,
        mesh=mesh,
        in_specs=placed,
        out_specs=(
            P(("seq", "wshard"), None),
            P(("seq", "wshard"), None),
            P(),
            P(None, "seq", "wshard"),
            P(None, "seq", "wshard"),
            P(),
            P(None, "seq", "wshard"),
            P(None, "wshard", "seq"),
        ),
        check_vma=False,
    )
```

profile of v0, /device:TPU:0, one launch (start us, length us, event | category | flops | bytes accessed | tf_op | source)
XLA Modules:
  0.0 1171.5 jit_solution(12835676939440190306)
XLA Ops:
  7.2 2.9 fusion.153
  18.3 64.7 %all-gather.17.cloned.1.call-done = bf16[1,768,2304]{1,2,0:T(8,128)(2,1)} async-done(((bf16[1,768,576]{1,2,0:T(8,128)(2,1)}), bf16[1,768,2304]{1,2,0:T(8,128)(2,1)}) %all-gather.17.cloned.1.call-update) | async-done | bytes 3538960 | tf_op jit(solution)/shard_map/all_gather | solution.py:158
  83.0 3.3 fusion.16
  98.8 7.2 collective-permute-done
  106.0 12.8 %collective-permute-done.1 = bf16[64,1536]{1,0:T(8,128)(2,1)S(1)} collective-permute-done((bf16[64,1536]{1,0:T(8,128)(2,1)S(1)}, bf16[64,1536]{1,0:T(8,128)(2,1)S(1)}, u32[]{:S(2)}, u32[]{:S(2)}) %collective-permute-start.1) | collective-permute-done | bytes 196640 | tf_op jit(solution)/shard_map/ppermute | solution.py:31
  130.8 62.4 %all-gather.21.cloned.1.call-done = bf16[1,768,2304]{1,2,0:T(8,128)(2,1)} async-done(((bf16[1,768,576]{1,2,0:T(8,128)(2,1)}), bf16[1,768,2304]{1,2,0:T(8,128)(2,1)}) %all-gather.21.cloned.1.call-update) | async-done | bytes 3538960 | tf_op jit(solution)/shard_map/all_gather | solution.py:160
  193.2 4.8 fusion.12
  198.0 36.1 %all-gather.23.cloned.1.call-done = bf16[1,1152,768]{2,1,0:T(8,128)(2,1)} async-done(((bf16[1,288,768]{2,1,0:T(8,128)(2,1)}), bf16[1,1152,768]{2,1,0:T(8,128)(2,1)}) %all-gather.23.cloned.1.call-update) | async-done | bytes 1769488 | tf_op jit(solution)/shard_map/all_gather | solution.py:161
  234.1 2.8 fusion.162
  238.5 65.8 %all-gather.25.cloned.1.call-done = bf16[1,768,2304]{1,2,0:T(8,128)(2,1)} async-done(((bf16[1,768,576]{1,2,0:T(8,128)(2,1)}), bf16[1,768,2304]{1,2,0:T(8,128)(2,1)}) %all-gather.25.cloned.1.call-update) | async-done | bytes 3538960 | tf_op jit(solution)/shard_map/all_gather | solution.py:158
  304.3 3.6 fusion.8
  328.5 5.8 collective-permute-done.2
  334.3 7.7 collective-permute-done.3
  357.1 53.2 %all-gather.29.cloned.1.call-done = bf16[1,768,2304]{1,2,0:T(8,128)(2,1)} async-done(((bf16[1,768,576]{1,2,0:T(8,128)(2,1)}), bf16[1,768,2304]{1,2,0:T(8,128)(2,1)}) %all-gather.29.cloned.1.call-update) | async-done | bytes 3538960 | tf_op jit(solution)/shard_map/all_gather | solution.py:160
  410.2 4.8 fusion.4
  415.1 35.6 %all-gather.31.cloned.1.call-done = bf16[1,1152,768]{2,1,0:T(8,128)(2,1)} async-done(((bf16[1,288,768]{2,1,0:T(8,128)(2,1)}), bf16[1,1152,768]{2,1,0:T(8,128)(2,1)}) %all-gather.31.cloned.1.call-update) | async-done | bytes 1769488 | tf_op jit(solution)/shard_map/all_gather | solution.py:161
  450.7 3.1 fusion.77
  463.1 4.4 fusion.108
  470.0 30.3 %fusion.29 = f32[12,64,320]{2,1,0:T(8,128)} fusion(bf16[192,12,64]{0,2,1:T(8,128)(2,1)} %fusion.93, f32[12,192,320]{2,1,0:T(8,128)} %fusion.164, f32[12,192,320]{2,1,0:T(8,128)} %copy-done, f32[12,192]{1,0:T(8,128)} %copy-done.75, pred[192,320]{1,0:T(8,128)(4,1)} %fusion.98), kind=kOutput, calls=%fused_computation.50 | convolution fusion | flops 102484544 | bytes 7246848 | tf_op jit(solution)/shard_map/hqk,qhd->khd/dot_general | solution.py:129
  500.3 3.0 fusion.27
  507.0 3.1 collective-permute-start.4
  511.3 19.6 %fusion.57 = f32[192,12,64]{0,2,1:T(8,128)} fusion(bf16[320,12,64]{0,2,1:T(8,128)(2,1)} %bitcast.189, f32[12,192,320]{2,1,0:T(8,128)} %fusion.164, f32[12,192,320]{2,1,0:T(8,128)} %copy-done, f32[12,192]{1,0:T(8,128)} %copy-done.75, pred[192,320]{1,0:T(8,128)(4,1)} %fusion.98), kind=kOutput, calls=%fused_computation.73 | convolution fusion | flops 102484544 | bytes 7050240 | tf_op jit(solution)/shard_map/hqk,khd->qhd/dot_general | solution.py:126
  535.4 5.0 scatter-add.14
  560.1 4.2 convolution_multiply_fusion.4
  564.3 4.2 convolution_multiply_fusion.5
  569.0 5.6 convolution_multiply_fusion
  575.3 5.6 convolution_multiply_fusion.2
  581.5 5.4 convolution_multiply_fusion.1
  591.4 3.6 fusion.165
  595.0 17.6 %fusion.35 = f32[12,64,320]{2,1,0:T(8,128)} fusion(bf16[192,12,64]{0,2,1:T(8,128)(2,1)} %fusion.91, f32[12,192,320]{2,1,0:T(8,128)} %fusion.165, f32[12,192,320]{2,1,0:T(8,128)S(1)} %get-tuple-element.149, f32[12,192]{1,0:T(8,128)} %copy-done.74, pred[192,320]{1,0:T(8,128)(4,1)} %fusion.98), kind=kOutput, calls=%fused_computation.52 | convolution fusion | flops 102484544 | bytes 7246848 | tf_op jit(solution)/shard_map/hqk,qhd->khd/dot_general | solution.py:129
  616.1 5.5 collective-permute-start.6
  624.7 17.0 %fusion.54 = f32[192,12,64]{0,2,1:T(8,128)} fusion(bf16[320,12,64]{0,2,1:T(8,128)(2,1)} %bitcast.185, f32[12,192,320]{2,1,0:T(8,128)} %fusion.165, f32[12,192,320]{2,1,0:T(8,128)S(1)} %get-tuple-element.149, f32[12,192]{1,0:T(8,128)} %copy-done.74, pred[192,320]{1,0:T(8,128)(4,1)} %fusion.98), kind=kOutput, calls=%fused_computation.72 | convolution fusion | flops 102484544 | bytes 7050240 | tf_op jit(solution)/shard_map/hqk,khd->qhd/dot_general | solution.py:126
  646.7 5.9 scatter-add.16
  656.5 4.2 convolution_multiply_fusion.3
  666.6 44.8 %reduce-scatter.45.cloned.1.call-done = f32[1152,96]{0,1:T(8,128)} async-done(((f32[1152,768]{0,1:T(8,128)}), f32[1152,96]{0,1:T(8,128)}) %reduce-scatter.45.cloned.1.call-update) | async-done | bytes 442384 | tf_op jit(solution)/shard_map/reduce_scatter | solution.py:321
  713.3 67.1 %reduce-scatter.43.cloned.1.call-done = f32[96,2304]{1,0:T(8,128)} async-done(((f32[768,2304]{1,0:T(8,128)}), f32[96,2304]{1,0:T(8,128)}) %reduce-scatter.43.cloned.1.call-update) | async-done | bytes 884752 | tf_op jit(solution)/shard_map/reduce_scatter | solution.py:320
  782.8 66.5 %reduce-scatter.35.cloned.1.call-done = f32[96,2304]{1,0:T(8,128)} async-done(((f32[768,2304]{1,0:T(8,128)}), f32[96,2304]{1,0:T(8,128)}) %reduce-scatter.35.cloned.1.call-update) | async-done | bytes 884752 | tf_op jit(solution)/shard_map/reduce_scatter | solution.py:318
  851.7 2.9 fusion.63
  854.7 63.5 %reduce-scatter.41.cloned.1.call-done = f32[96,2304]{1,0:T(8,128)} async-done(((f32[768,2304]{1,0:T(8,128)}), f32[96,2304]{1,0:T(8,128)}) %reduce-scatter.41.cloned.1.call-update) | async-done | bytes 884752 | tf_op jit(solution)/shard_map/reduce_scatter | solution.py:320
  920.8 3.1 multiply_reduce_fusion.5
  923.9 63.2 %reduce-scatter.33.cloned.1.call-done = f32[96,2304]{1,0:T(8,128)} async-done(((f32[768,2304]{1,0:T(8,128)}), f32[96,2304]{1,0:T(8,128)}) %reduce-scatter.33.cloned.1.call-update) | async-done | bytes 884752 | tf_op jit(solution)/shard_map/reduce_scatter | solution.py:318
  989.5 39.8 %all-reduce = (f32[2,768]{1,0:T(2,128)}, f32[2,768]{1,0:T(2,128)}) all-reduce(f32[2,768]{1,0:T(2,128)S(1)} %pad_maximum_fusion.24, f32[2,768]{1,0:T(2,128)S(1)} %pad_maximum_fusion.25), channel_id=1, replica_groups=mesh['seq'=8,'wshard'=4] {'seq','wshard'}, use_global_device_ids=true, to_apply=%region_24.25 | all-reduce | flops 3072 | bytes 24576 | tf_op jit(solution)/shard_map/psum | solution.py:341
  1032.9 17.8 %reduce-scatter.63.cloned.1.call-done = bf16[288,96]{1,0:T(8,128)(2,1)} async-done(((bf16[1152,96]{1,0:T(8,128)(2,1)}), bf16[288,96]{1,0:T(8,128)(2,1)}) %reduce-scatter.63.cloned.1.call-update) | async-done | bytes 55312
  1051.7 19.6 %reduce-scatter.61.cloned.1.call-done = bf16[288,96]{1,0:T(8,128)(2,1)} async-done(((bf16[1152,96]{1,0:T(8,128)(2,1)}), bf16[288,96]{1,0:T(8,128)(2,1)}) %reduce-scatter.61.cloned.1.call-update) | async-done | bytes 55312
  1073.2 20.8 %reduce-scatter.59.cloned.1.call-done = bf16[576,96]{1,0:T(8,128)(2,1)} async-done(((bf16[2304,96]{1,0:T(8,128)(2,1)}), bf16[576,96]{1,0:T(8,128)(2,1)}) %reduce-scatter.59.cloned.1.call-update) | async-done | bytes 110608
  1095.1 21.8 %reduce-scatter.51.cloned.1.call-done = bf16[576,96]{1,0:T(8,128)(2,1)} async-done(((bf16[2304,96]{1,0:T(8,128)(2,1)}), bf16[576,96]{1,0:T(8,128)(2,1)}) %reduce-scatter.51.cloned.1.call-update) | async-done | bytes 110608
  1117.9 21.8 %reduce-scatter.57.cloned.1.call-done = bf16[576,96]{1,0:T(8,128)(2,1)} async-done(((bf16[2304,96]{1,0:T(8,128)(2,1)}), bf16[576,96]{1,0:T(8,128)(2,1)}) %reduce-scatter.57.cloned.1.call-update) | async-done | bytes 110608
  1141.7 20.9 %reduce-scatter.49.cloned.1.call-done = bf16[576,96]{1,0:T(8,128)(2,1)} async-done(((bf16[2304,96]{1,0:T(8,128)(2,1)}), bf16[576,96]{1,0:T(8,128)(2,1)}) %reduce-scatter.49.cloned.1.call-update) | async-done | bytes 110608
  (417 shorter events, 161.2 us)
Async XLA Ops:
  7.2 75.8 %all-gather.17.cloned.1.call-start = ((), (), s32[]{:S(2)}) async-start(), calls=%async_computation.24 | async-start | bytes 4423680 | tf_op jit(solution)/shard_map/all_gather | solution.py:158
  10.2 116.8 %all-gather.19.cloned.1.call-start = ((), (), s32[]{:S(2)}) async-start(), calls=%async_computation.25 | async-start | bytes 1474560 | tf_op jit(solution)/shard_map/all_gather | solution.py:159
  11.1 182.1 %all-gather.21.cloned.1.call-start = ((), (), s32[]{:S(2)}) async-start(), calls=%async_computation.26 | async-start | bytes 4423680 | tf_op jit(solution)/shard_map/all_gather | solution.py:160
  12.6 221.5 %all-gather.23.cloned.1.call-start = ((), (), s32[]{:S(2)}) async-start(), calls=%async_computation.27 | async-start | bytes 2211840 | tf_op jit(solution)/shard_map/all_gather | solution.py:161
  13.6 290.7 %all-gather.25.cloned.1.call-start = ((), (), s32[]{:S(2)}) async-start(), calls=%async_computation.28 | async-start | bytes 4423680 | tf_op jit(solution)/shard_map/all_gather | solution.py:158
  14.2 339.1 %all-gather.27.cloned.1.call-start = ((), (), s32[]{:S(2)}) async-start(), calls=%async_computation.29 | async-start | bytes 1474560 | tf_op jit(solution)/shard_map/all_gather | solution.py:159
  14.8 395.5 %all-gather.29.cloned.1.call-start = ((), (), s32[]{:S(2)}) async-start(), calls=%async_computation.30 | async-start | bytes 4423680 | tf_op jit(solution)/shard_map/all_gather | solution.py:160
  15.5 435.1 %all-gather.31.cloned.1.call-start = ((), (), s32[]{:S(2)}) async-start(), calls=%async_computation.31 | async-start | bytes 2211840 | tf_op jit(solution)/shard_map/all_gather | solution.py:161
  16.3 644.4 %reduce-scatter.39.cloned.1.call-start = ((), (), s32[]{:S(2)}) async-start(), calls=%async_computation.19 | async-start | bytes 2654208 | tf_op jit(solution)/shard_map/reduce_scatter | solution.py:319
  16.5 69.8 %copy-start.81 = (f32[192]{0:T(256)}, f32[192]{0:T(256)S(1)}, u32[]{:S(2)}) copy-start(f32[192]{0:T(256)S(1)} %broadcast_multiply_fusion.19) | copy-start | bytes 2308
  16.8 69.6 %copy-start.89 = (f32[192]{0:T(256)}, f32[192]{0:T(256)S(1)}, u32[]{:S(2)}) copy-start(f32[192]{0:T(256)S(1)} %add_rsqrt_fusion.3) | copy-start | bytes 2308
  17.1 80.8 %copy-start.32 = (f32[192,64]{0,1:T(8,128)}, f32[192,64]{0,1:T(8,128)S(1)}, u32[]{:S(2)}) copy-start(f32[192,64]{0,1:T(8,128)S(1)} %pad_maximum_fusion.22) | copy-start | bytes 147460
  17.1 80.8 %copy-start.42 = (f32[192,64]{0,1:T(8,128)}, f32[192,64]{0,1:T(8,128)S(1)}, u32[]{:S(2)}) copy-start(f32[192,64]{0,1:T(8,128)S(1)} %pad_maximum_fusion.23) | copy-start | bytes 147460
  17.4 74.5 %copy-start.30 = (f32[192,768]{1,0:T(8,128)}, f32[192,768]{1,0:T(8,128)S(1)}, u32[]{:S(2)}) copy-start(f32[192,768]{1,0:T(8,128)S(1)} %copy.67) | copy-start | bytes 1769476
  94.2 24.6 %copy-start.50 = (bf16[192,768]{1,0:T(8,128)(2,1)S(1)}, bf16[192,768]{1,0:T(8,128)(2,1)}, u32[]{:S(2)}) copy-start(bf16[192,768]{1,0:T(8,128)(2,1)} %slice.501) | copy-start | bytes 884740
  95.2 10.8 collective-permute-start
  96.5 22.3 %collective-permute-start.1 = (bf16[64,1536]{1,0:T(8,128)(2,1)S(1)}, bf16[64,1536]{1,0:T(8,128)(2,1)S(1)}, u32[]{:S(2)}, u32[]{:S(2)}) collective-permute-start(bf16[64,1536]{1,0:T(8,128)(2,1)S(1)} %get-tuple-element.141), channel_id=1, source_target_pairs={{1,0},{2,1},{3,2},{4,3},{5,4},{6,5},{7,6},{8,7},{9,8},{10,9},{11,1... | collective-permute-start | bytes 589832 | tf_op jit(solution)/shard_map/ppermute | solution.py:31
  322.3 19.6 %copy-start.48 = (bf16[192,768]{1,0:T(8,128)(2,1)S(1)}, bf16[192,768]{1,0:T(8,128)(2,1)}, u32[]{:S(2)}) copy-start(bf16[192,768]{1,0:T(8,128)(2,1)} %get-tuple-element.105) | copy-start | bytes 884740
  322.3 19.6 %copy-start.49 = (bf16[192,768]{1,0:T(8,128)(2,1)S(1)}, bf16[192,768]{1,0:T(8,128)(2,1)}, u32[]{:S(2)}) copy-start(bf16[192,768]{1,0:T(8,128)(2,1)} %slice.500) | copy-start | bytes 884740
  323.5 10.8 collective-permute-start.2
  324.8 17.1 %collective-permute-start.3 = (bf16[64,1536]{1,0:T(8,128)(2,1)S(1)}, bf16[64,1536]{1,0:T(8,128)(2,1)S(1)}, u32[]{:S(2)}, u32[]{:S(2)}) collective-permute-start(bf16[64,1536]{1,0:T(8,128)(2,1)S(1)} %get-tuple-element.139), channel_id=1, source_target_pairs={{1,0},{2,1},{3,2},{4,3},{5,4},{6,5},{7,6},{8,7},{9,8},{10,9},{11,1... | collective-permute-start | bytes 589832 | tf_op jit(solution)/shard_map/ppermute | solution.py:31
  504.9 157.7 %reduce-scatter.37.cloned.1.call-start = ((), (), s32[]{:S(2)}) async-start(), calls=%async_computation.18 | async-start | bytes 2654208 | tf_op jit(solution)/shard_map/reduce_scatter | solution.py:319
  507.0 24.0 %collective-permute-start.4 = (bf16[64,1536]{0,1:T(8,128)(2,1)}, bf16[64,1536]{0,1:T(8,128)(2,1)}, u32[]{:S(2)}, u32[]{:S(2)}) collective-permute-start(bf16[64,1536]{0,1:T(8,128)(2,1)} %get-tuple-element.112), channel_id=1, source_target_pairs={{0,1},{1,2},{2,3},{3,4},{4,5},{5,6},{6,7},{7,8},{8,9},{9,10},{10,1... | collective-permute-start | bytes 589832 | tf_op jit(solution)/shard_map/ppermute | solution.py:29
  510.1 20.9 %collective-permute-start.5 = (bf16[64,1536]{0,1:T(8,128)(2,1)}, bf16[64,1536]{0,1:T(8,128)(2,1)}, u32[]{:S(2)}, u32[]{:S(2)}) collective-permute-start(bf16[64,1536]{0,1:T(8,128)(2,1)} %get-tuple-element.113), channel_id=1, source_target_pairs={{1,0},{2,1},{3,2},{4,3},{5,4},{6,5},{7,6},{8,7},{9,8},{10,9},{11,1... | collective-permute-start | bytes 589832 | tf_op jit(solution)/shard_map/ppermute | solution.py:31
  560.0 104.5 %reduce-scatter.47.cloned.1.call-start = ((), (), s32[]{:S(2)}) async-start(), calls=%async_computation.23 | async-start | bytes 3981312 | tf_op jit(solution)/shard_map/reduce_scatter | solution.py:321
  564.3 147.1 %reduce-scatter.45.cloned.1.call-start = ((), (), s32[]{:S(2)}) async-start(), calls=%async_computation.22 | async-start | bytes 3981312 | tf_op jit(solution)/shard_map/reduce_scatter | solution.py:321
  568.5 211.8 %reduce-scatter.43.cloned.1.call-start = ((), (), s32[]{:S(2)}) async-start(), calls=%async_computation.21 | async-start | bytes 7962624 | tf_op jit(solution)/shard_map/reduce_scatter | solution.py:320
  574.6 274.7 %reduce-scatter.35.cloned.1.call-start = ((), (), s32[]{:S(2)}) async-start(), calls=%async_computation.17 | async-start | bytes 7962624 | tf_op jit(solution)/shard_map/reduce_scatter | solution.py:318
  580.9 337.3 %reduce-scatter.41.cloned.1.call-start = ((), (), s32[]{:S(2)}) async-start(), calls=%async_computation.20 | async-start | bytes 7962624 | tf_op jit(solution)/shard_map/reduce_scatter | solution.py:320
  586.9 400.2 %reduce-scatter.33.cloned.1.call-start = ((), (), s32[]{:S(2)}) async-start(), calls=%async_computation.16 | async-start | bytes 7962624 | tf_op jit(solution)/shard_map/reduce_scatter | solution.py:318
  614.8 8.2 copy-start.12
  616.1 25.6 %collective-permute-start.6 = (bf16[64,1536]{0,1:T(8,128)(2,1)}, bf16[64,1536]{0,1:T(8,128)(2,1)}, u32[]{:S(2)}, u32[]{:S(2)}) collective-permute-start(bf16[64,1536]{0,1:T(8,128)(2,1)} %get-tuple-element.110), channel_id=1, source_target_pairs={{0,1},{1,2},{2,3},{3,4},{4,5},{5,6},{6,7},{7,8},{8,9},{9,10},{10,1... | collective-permute-start | bytes 589832 | tf_op jit(solution)/shard_map/ppermute | solution.py:29
  621.6 20.5 %collective-permute-start.7 = (bf16[64,1536]{0,1:T(8,128)(2,1)}, bf16[64,1536]{0,1:T(8,128)(2,1)}, u32[]{:S(2)}, u32[]{:S(2)}) collective-permute-start(bf16[64,1536]{0,1:T(8,128)(2,1)} %get-tuple-element.111), channel_id=1, source_target_pairs={{1,0},{2,1},{3,2},{4,3},{5,4},{6,5},{7,6},{8,7},{9,8},{10,9},{11,1... | collective-permute-start | bytes 589832 | tf_op jit(solution)/shard_map/ppermute | solution.py:31
  660.6 369.7 %reduce-scatter.55.cloned.1.call-start = ((), (), s32[]{:S(2)}) async-start(), calls=%async_computation.35 | async-start | bytes 245760
  662.5 368.7 %reduce-scatter.53.cloned.1.call-start = ((), (), s32[]{:S(2)}) async-start(), calls=%async_computation.34 | async-start | bytes 245760
  664.5 386.2 %reduce-scatter.63.cloned.1.call-start = ((), (), s32[]{:S(2)}) async-start(), calls=%async_computation.39 | async-start | bytes 368640
  666.5 404.8 %reduce-scatter.61.cloned.1.call-start = ((), (), s32[]{:S(2)}) async-start(), calls=%async_computation.38 | async-start | bytes 368640
  713.3 380.7 %reduce-scatter.59.cloned.1.call-start = ((), (), s32[]{:S(2)}) async-start(), calls=%async_computation.37 | async-start | bytes 737280
  781.6 70.0 %copy-start.94 = (f32[768]{0:T(1024)S(1)}, f32[768]{0:T(1024)}, u32[]{:S(2)}) copy-start(f32[768]{0:T(1024)} %get-tuple-element.82) | copy-start | bytes 9220
  781.6 70.1 %copy-start.5 = (f32[192,768]{1,0:T(8,128)S(1)}, f32[192,768]{1,0:T(8,128)}, u32[]{:S(2)}) copy-start(f32[192,768]{1,0:T(8,128)} %copy-done.3) | copy-start | bytes 1769476
  781.6 70.1 %copy-start.26 = (f32[192,2304]{1,0:T(8,128)S(1)}, f32[192,2304]{1,0:T(8,128)}, u32[]{:S(2)}) copy-start(f32[192,2304]{1,0:T(8,128)} %fusion.4) | copy-start | bytes 5308420
  782.7 334.2 %reduce-scatter.51.cloned.1.call-start = ((), (), s32[]{:S(2)}) async-start(), calls=%async_computation.33 | async-start | bytes 737280
  851.6 288.2 %reduce-scatter.57.cloned.1.call-start = ((), (), s32[]{:S(2)}) async-start(), calls=%async_computation.36 | async-start | bytes 737280
  854.6 66.2 %copy-start.58 = (bf16[192,768]{0,1:T(8,128)(2,1)S(1)}, bf16[192,768]{0,1:T(8,128)(2,1)}, u32[]{:S(2)}) copy-start(bf16[192,768]{0,1:T(8,128)(2,1)} %copy-done.57) | copy-start | bytes 884740
  854.6 66.2 %copy-start.61 = (bf16[192,768]{0,1:T(8,128)(2,1)S(1)}, bf16[192,768]{0,1:T(8,128)(2,1)}, u32[]{:S(2)}) copy-start(bf16[192,768]{0,1:T(8,128)(2,1)} %copy-done.60) | copy-start | bytes 884740
  854.6 66.2 %copy-start.63 = (bf16[192,12,64]{0,2,1:T(8,128)(2,1)S(1)}, bf16[192,12,64]{0,2,1:T(8,128)(2,1)}, u32[]{:S(2)}) copy-start(bf16[192,12,64]{0,2,1:T(8,128)(2,1)} %copy-done.62) | copy-start | bytes 884740
  920.5 242.0 %reduce-scatter.49.cloned.1.call-start = ((), (), s32[]{:S(2)}) async-start(), calls=%async_computation.32 | async-start | bytes 737280
  923.9 105.4 %copy-start.21 = (f32[192,768]{1,0:T(8,128)S(1)}, f32[192,768]{1,0:T(8,128)}, u32[]{:S(2)}) copy-start(f32[192,768]{1,0:T(8,128)} %copy-done.20) | copy-start | bytes 1769476
  (81 other events, 184.1 us)
Sparse Core Ops, SparseCore 0:
  10.3 72.6 all-gather.16
  85.1 37.2 all-gather.18
  124.0 69.1 all-gather.20
  195.2 38.8 all-gather.22
  235.5 68.7 all-gather.24
  305.7 35.4 all-gather.26
  342.8 67.4 all-gather.28
  411.8 38.8 all-gather.30
  505.0 41.9 reduce-scatter.38
  560.1 44.0 reduce-scatter.36
  607.7 52.2 reduce-scatter.46
  663.3 47.9 reduce-scatter.44
  714.8 65.4 reduce-scatter.42
  783.8 65.4 reduce-scatter.34
  852.7 65.4 reduce-scatter.40
  921.6 65.5 reduce-scatter.32
  989.8 19.6 reduce-scatter.54
  1011.6 17.7 reduce-scatter.52
  1032.2 18.4 reduce-scatter.62
  1052.8 18.4 reduce-scatter.60
  1073.6 20.3 reduce-scatter.58
  1096.3 20.5 reduce-scatter.50
  1119.2 20.5 reduce-scatter.56
  1141.9 20.5 reduce-scatter.48
where the time goes:
time: 1180 us; the launch traced here: 1170 us
  waiting for transfers between devices  782 us (66%)
  matrix products  182 us (15%)
  local copies, waits for them, and re-layouts  82.5 us (7%)
  other arithmetic  51 us (4%)
  blocking collectives  39.8 us (3%)
  starting transfers between devices  18.3 us (2%)
  between operations  16 us (1%)
    reduce_scatter x2, waiting for transfers between devices, per_device(): lax.psum_scatter(local_in, 'seq', scatter_dimension=0, tiled=True)  131 us
    all_gather x2, waiting for transfers between devices, per_device(): lax.all_gather(qkv_weight[layer_number], 'wshard', axis=1, tiled=True)  130 us
    reduce_scatter x2, waiting for transfers between devices, per_device(): lax.psum_scatter(local_qkv, 'seq', scatter_dimension=0, tiled=True)  130 us
    unnamed x32, waiting for transfers between devices  126 us
    all_gather x2, waiting for transfers between devices, per_device(): lax.all_gather(input_weight[layer_number], 'wshard', axis=1, tiled=True)  116 us
    all_gather x2, waiting for transfers between devices, per_device(): lax.all_gather(down_weight[layer_number], 'wshard', axis=0, tiled=True)  71.7 us
    dot_general x2, matrix products, attend_backward(): jnp.einsum('hqk,qhd->khd', grad_scores, query_matrix, preferred_element_t...  47.9 us
    reduce_scatter x2, waiting for transfers between devices, per_device(): lax.psum_scatter(local_down, 'seq', scatter_dimension=1, tiled=True)  44.8 us
  transfers between devices with their start and end apart: 32, of which 22 were waited for; matrix products, arithmetic and copies ran while one was open for 20% of the time, Pallas kernels for 0%

commit v1 on v0

--- a/solution.py
+++ b/solution.py
@@ -130,6 +130,31 @@
         "hqk,qhd->khd", grad_scores, query_matrix, preferred_element_type=jnp.float32
     )
     return (grad_queries, grad_keys, grad_values)
+
+
+def gather_all(share, n_w, n_seq):
+    whole = lax.all_gather(share, ("wshard", "seq"), axis=0, tiled=False)
+    return whole.reshape(n_w, n_seq * share.shape[0], share.shape[1])
+
+
+def sum_over_blocks(terms, n_w, n_seq):
+    depth = terms.shape[1] // n_seq
+    parts = terms.reshape(n_w, n_seq, depth, terms.shape[2]).transpose(1, 0, 2, 3)
+    return lax.psum_scatter(parts, "seq", scatter_dimension=0, tiled=True)[0]
+
+
+def sum_everywhere(values, axes):
+    for axis in axes:
+        count = lax.axis_size(axis)
+        if count & (count - 1):
+            values = lax.psum(values, axis)
+            continue
+        step = 1
+        while step < count:
+            pairs = [(i, i ^ step) for i in range(count)]
+            values = values + lax.ppermute(values, axis, pairs)
+            step *= 2
+    return values
 
 
 def per_device(
@@ -151,21 +176,74 @@
     allowed = band_mask(query_pos, key_pos, length)
     cosine, sine = rope_tables(query_pos % length)
     scale_grad = 1.0 / math.sqrt(total_tokens)
+    n_seq = lax.axis_size("seq")
+    n_w = lax.axis_size("wshard")
+    strip = D // n_seq
+    seq_index = lax.axis_index("seq")
+    col_qkv = qkv_weight.shape[2]
+    col_out = output_weight.shape[2]
+    col_in = input_weight.shape[2]
+    row_down = down_weight.shape[1]
+
+    def own_strip(weight, axis):
+        return lax.dynamic_slice_in_dim(weight, seq_index * strip, strip, axis)
+
+    gathered = []
+    for layer_number in range(LAYERS):
+        share = jnp.concatenate(
+            [
+                own_strip(qkv_weight[layer_number], 0),
+                own_strip(input_weight[layer_number], 0),
+                own_strip(down_weight[layer_number], 1).T,
+                own_strip(output_weight[layer_number], 0),
+            ],
+            axis=1,
+        )
+        whole = gather_all(share, n_w, n_seq)
+        ends = (col_qkv, col_qkv + col_in, col_qkv + col_in + row_down)
+        gathered.append(
+            (
+                whole[:, :, : ends[0]],
+                whole[:, :, ends[0] : ends[1]],
+                whole[:, :, ends[1] : ends[2]],
+                whole[:, :, ends[2] :],
+            )
+        )
+
+    def columns_product(left, weight):
+        return jnp.concatenate(
+            [jnp.dot(left, weight[i], preferred_element_type=jnp.float32) for i in range(n_w)],
+            axis=1,
+        )
+
+    def rows_product(left, weight):
+        return jnp.einsum(
+            "twf,wdf->td",
+            left.reshape(rows, n_w, weight.shape[2]),
+            weight,
+            preferred_element_type=jnp.float32,
+        )
+
+    def blocks(left, right, width):
+        return (
+            jnp.einsum(
+                "td,twf->wdf",
+                left,
+                right.reshape(rows, n_w, width),
+                preferred_element_type=jnp.float32,
+            )
+            * scale_grad
+        ).astype(jnp.bfloat16)
+
     hidden_state = tokens
     saved_activations = []
     for layer_number in range(LAYERS):
-        gathered = (
-            lax.all_gather(qkv_weight[layer_number], "wshard", axis=1, tiled=True),
-            lax.all_gather(output_weight[layer_number], "wshard", axis=1, tiled=True),
-            lax.all_gather(input_weight[layer_number], "wshard", axis=1, tiled=True),
-            lax.all_gather(down_weight[layer_number], "wshard", axis=0, tiled=True),
-        )
-        full_qkv, full_out, full_in, full_down = gathered
+        full_qkv, full_in, full_down, full_out = gathered[layer_number]
         attention_standardized, attention_inverse_deviation = layer_normalize(hidden_state)
         attention_normalized = (attention_standardized * attention_norm_gain[layer_number]).astype(
             jnp.bfloat16
         )
-        qkv = jnp.dot(attention_normalized, full_qkv, preferred_element_type=jnp.float32)
+        qkv = columns_product(attention_normalized, full_qkv)
         query_matrix = apply_rope(qkv[:, :D].reshape(rows, HEADS, HDIM), cosine, sine).astype(
             jnp.bfloat16
         )
@@ -182,16 +260,12 @@
         padded_values = edged[:, D:].reshape(rows + 2 * WIN, HEADS, HDIM)
         context_rows, log_total = attend_forward(query_matrix, padded_keys, padded_values, allowed)
         context_rows = context_rows.reshape(rows, D)
-        middle_state = hidden_state + jnp.dot(
-            context_rows, full_out, preferred_element_type=jnp.float32
-        )
+        middle_state = hidden_state + columns_product(context_rows, full_out)
         feedforward_standardized, feedforward_inverse_deviation = layer_normalize(middle_state)
         feedforward_normalized = (
             feedforward_standardized * feedforward_norm_gain[layer_number]
         ).astype(jnp.bfloat16)
-        inner_activation = jnp.dot(
-            feedforward_normalized, full_in, preferred_element_type=jnp.float32
-        )
+        inner_activation = columns_product(feedforward_normalized, full_in)
         gated_linear_output = (
             gelu_exact(inner_activation[:, :FF]) * inner_activation[:, FF:]
         ).astype(jnp.bfloat16)
@@ -214,11 +288,9 @@
                 gated_linear_output,
             )
         )
-        hidden_state = middle_state + jnp.dot(
-            gated_linear_output, full_down, preferred_element_type=jnp.float32
-        )
+        hidden_state = middle_state + rows_product(gated_linear_output, full_down)
     grad = cotangent
-    list_again, list_qkv, list_out, list_fgain, list_in, list_down = ([], [], [], [], [], [])
+    list_again, list_fgain, block_sums = ([], [], [])
     for layer_number in reversed(range(LAYERS)):
         (
             holding,
@@ -236,28 +308,23 @@
             inner_activation,
             gated_linear_output,
         ) = saved_activations[layer_number]
-        full_qkv, full_out, full_in, full_down = (
-            lax.all_gather(qkv_weight[layer_number], "wshard", axis=1, tiled=True),
-            lax.all_gather(output_weight[layer_number], "wshard", axis=1, tiled=True),
-            lax.all_gather(input_weight[layer_number], "wshard", axis=1, tiled=True),
-            lax.all_gather(down_weight[layer_number], "wshard", axis=0, tiled=True),
-        )
+        full_qkv, full_in, full_down, full_out = gathered[layer_number]
         grad_rounded = grad.astype(jnp.bfloat16)
-        local_down = (
-            jnp.dot(gated_linear_output.T, grad_rounded, preferred_element_type=jnp.float32)
-            * scale_grad
-        )
-        grad_geglu = jnp.dot(grad_rounded, full_down.T, preferred_element_type=jnp.float32)
+        local_down = blocks(grad_rounded, gated_linear_output, row_down)
+        grad_geglu = columns_product(grad_rounded, full_down)
         gate = inner_activation[:, :FF]
         upper = inner_activation[:, FF:]
         grad_inner = jnp.concatenate(
             [grad_geglu * upper * gelu_slope(gate), grad_geglu * gelu_exact(gate)], axis=1
         ).astype(jnp.bfloat16)
-        local_in = (
-            jnp.dot(feedforward_normalized.T, grad_inner, preferred_element_type=jnp.float32)
-            * scale_grad
-        )
-        normalized_gradient = jnp.dot(grad_inner, full_in.T, preferred_element_type=jnp.float32)
+        local_in = blocks(feedforward_normalized, grad_inner, col_in)
+        feed_terms = [local_in, local_down]
+        if layer_number == 0:
+            block_sums.append(
+                sum_over_blocks(jnp.concatenate(feed_terms, axis=2), n_w, n_seq)
+            )
+            feed_terms = []
+        normalized_gradient = rows_product(grad_inner, full_in)
         partial_gradient, feedforward_gain_gradient = norm_backward_step(
             normalized_gradient,
             feedforward_standardized,
@@ -267,12 +334,9 @@
         list_fgain.append(feedforward_gain_gradient * scale_grad)
         grad_middle = grad + partial_gradient
         grad_middle_rounded = grad_middle.astype(jnp.bfloat16)
-        local_out = (
-            jnp.dot(context_rows.T, grad_middle_rounded, preferred_element_type=jnp.float32)
-            * scale_grad
-        )
+        local_out = blocks(context_rows, grad_middle_rounded, col_out)
         grad_context = (
-            jnp.dot(grad_middle_rounded, full_out.T, preferred_element_type=jnp.float32)
+            rows_product(grad_middle_rounded, full_out)
             .astype(jnp.bfloat16)
             .reshape(rows, HEADS, HDIM)
         )
@@ -299,13 +363,13 @@
             ],
             axis=1,
         ).astype(jnp.bfloat16)
-        local_qkv = (
-            jnp.dot(attention_normalized.T, grad_qkv, preferred_element_type=jnp.float32)
-            * scale_grad
-        )
-        attention_normalized_gradient = jnp.dot(
-            grad_qkv, full_qkv.T, preferred_element_type=jnp.float32
-        )
+        local_qkv = blocks(attention_normalized, grad_qkv, col_qkv)
+        block_sums.append(
+            sum_over_blocks(
+                jnp.concatenate(feed_terms + [local_qkv, local_out], axis=2), n_w, n_seq
+            )
+        )
+        attention_normalized_gradient = rows_product(grad_qkv, full_qkv)
         attention_partial_gradient, attention_gain_gradient = norm_backward_step(
             attention_normalized_gradient,
             attention_standardized,
@@ -314,42 +378,31 @@
         )
         list_again.append(attention_gain_gradient * scale_grad)
         grad = grad_middle + attention_partial_gradient
-        partial_sums = (
-            lax.psum_scatter(local_qkv, "seq", scatter_dimension=0, tiled=True),
-            lax.psum_scatter(local_out, "seq", scatter_dimension=0, tiled=True),
-            lax.psum_scatter(local_in, "seq", scatter_dimension=0, tiled=True),
-            lax.psum_scatter(local_down, "seq", scatter_dimension=1, tiled=True),
-        )
-        reduced = (
-            lax.psum_scatter(
-                partial_sums[0].astype(jnp.bfloat16), "wshard", scatter_dimension=1, tiled=True
-            ).astype(jnp.float32),
-            lax.psum_scatter(
-                partial_sums[1].astype(jnp.bfloat16), "wshard", scatter_dimension=1, tiled=True
-            ).astype(jnp.float32),
-            lax.psum_scatter(
-                partial_sums[2].astype(jnp.bfloat16), "wshard", scatter_dimension=1, tiled=True
-            ).astype(jnp.float32),
-            lax.psum_scatter(
-                partial_sums[3].astype(jnp.bfloat16), "wshard", scatter_dimension=0, tiled=True
-            ).astype(jnp.float32),
-        )
-        list_qkv.append(reduced[0])
-        list_out.append(reduced[1])
-        list_in.append(reduced[2])
-        list_down.append(reduced[3])
-    gain_sums = lax.psum(
-        (jnp.stack(list_again[::-1]), jnp.stack(list_fgain[::-1])), ("seq", "wshard")
-    )
+    gain_sums = sum_everywhere(
+        jnp.concatenate([jnp.stack(list_again[::-1]), jnp.stack(list_fgain[::-1])], axis=0),
+        ("seq", "wshard"),
+    )
+    summed = lax.psum_scatter(
+        jnp.concatenate(block_sums, axis=2), "wshard", scatter_dimension=0, tiled=True
+    )[0].astype(jnp.float32)
+    per_layer = (col_in, row_down, col_qkv, col_out)
+    pieces = []
+    start = 0
+    for width in per_layer * LAYERS:
+        pieces.append(summed[:, start : start + width])
+        start += width
+    by_kind = [
+        jnp.stack([pieces[4 * (LAYERS - 1 - n) + kind] for n in range(LAYERS)]) for kind in range(4)
+    ]
     return (
         hidden_state,
         grad,
-        gain_sums[0],
-        jnp.stack(list_qkv[::-1]),
-        jnp.stack(list_out[::-1]),
-        gain_sums[1],
-        jnp.stack(list_in[::-1]),
-        jnp.stack(list_down[::-1]),
+        gain_sums[:LAYERS],
+        by_kind[2],
+        by_kind[3],
+        gain_sums[LAYERS:],
+        by_kind[0],
+        jnp.swapaxes(by_kind[1], 1, 2),
     )
 
 

time: 1180 us -> 933 us (0.79)
  waiting for transfers between devices: 782 us -> 474 us
  local copies, waits for them, and re-layouts: 82.5 us -> 132 us
  blocking collectives: 39.8 us -> 0 us
  matrix products: 182 us -> 205 us
  other arithmetic: 51 us -> 70.9 us
    reduce_scatter x8 -> x1, waiting for transfers between devices: 305 us -> 25.5 us  [per_device(): lax.psum_scatter(jnp.concatenate(block_sums, axis=2), 'wshard', scatter_d...]
    all_gather x8 -> x2, waiting for transfers between devices: 318 us -> 164 us  [gather_all(): whole = lax.all_gather(share, ('wshard', 'seq'), axis=0, tiled=False)]
    unnamed x32 -> x5, waiting for transfers between devices: 126 us -> 258 us
    concatenate x0 -> x18, local copies, waits for them, and re-layouts: none -> 61.7 us  [the longest x12 27.2 us: columns_product(): jnp.concatenate([jnp.dot(left, weight[i], preferred_element_type=jnp.floa...]
    psum x1 -> x0, blocking collectives: 39.8 us -> none  [per_device(): lax.psum((jnp.stack(list_again[::-1]), jnp.stack(list_fgain[::-1])), ('se...]
    dot_general x24 -> x48, matrix products: 76.3 us -> 114 us  [the longest x32 64.6 us: columns_product(): jnp.dot(left, weight[i], preferred_element_type=jnp.float32)]
    unnamed x211 -> x226, local copies, waits for them, and re-layouts: 35.2 us -> 11.7 us
    concatenate x0 -> x10, other arithmetic: none -> 18.8 us  [the longest x2 9.39 us: per_device(): jnp.concatenate(feed_terms + [local_qkv, local_out], axis=2)]
  transfers between devices with their start and end apart: 32 -> 17, of which waited for: 22 -> 13; matrix products, arithmetic and copies ran while one was open for 20% -> 7% of each run, Pallas kernels for 0% -> 0%
where the time goes in v1:
time: 933 us; the launch traced here: 924 us
  waiting for transfers between devices  474 us (51%)
  matrix products  205 us (22%)
  local copies, waits for them, and re-layouts  132 us (14%)
  other arithmetic  70.9 us (8%)
  starting transfers between devices  26.2 us (3%)
  between operations  15.7 us (2%)
    unnamed x5, waiting for transfers between devices  258 us
    all_gather x2, waiting for transfers between devices, gather_all(): whole = lax.all_gather(share, ('wshard', 'seq'), axis=0, tiled=False)  164 us
    dot_general x32, matrix products, columns_product(): jnp.dot(left, weight[i], preferred_element_type=jnp.float32)  64.6 us
    dot_general x2, matrix products, attend_backward(): jnp.einsum('hqk,qhd->khd', grad_scores, query_matrix, preferred_element_t...  36.6 us
    dot_general x2, matrix products, attend_backward(): jnp.einsum('hqk,khd->qhd', grad_scores, padded_keys, preferred_element_ty...  35.7 us
    dot_general x8, matrix products, rows_product(): jnp.einsum('twf,wdf->td', left.reshape(rows, n_w, weight.shape[2]), weigh...  32 us
    concatenate x12, local copies, waits for them, and re-layouts, columns_product(): jnp.concatenate([jnp.dot(left, weight[i], preferred_element_type=jnp.floa...  27.2 us
    reduce_scatter x1, waiting for transfers between devices, per_device(): lax.psum_scatter(jnp.concatenate(block_sums, axis=2), 'wshard', scatter_d...  25.5 us
  transfers between devices with their start and end apart: 17, of which 13 were waited for; matrix products, arithmetic and copies ran while one was open for 7% of the time, Pallas kernels for 0%

profile of v1, /device:TPU:0, one launch (start us, length us, event | category | flops | bytes accessed | tf_op | source)
XLA Modules:
  0.0 923.8 jit_solution(7029571634951242276)
XLA Ops:
  25.5 81.3 %all-gather.7.cloned.1.call-done = bf16[3072,1632]{1,0:T(8,128)(2,1)} async-done(((bf16[96,1632]{1,0:T(8,128)(2,1)}), bf16[3072,1632]{1,0:T(8,128)(2,1)}) %all-gather.7.cloned.1.call-update) | async-done | bytes 10027024 | tf_op jit(solution)/shard_map/all_gather | solution.py:136
  110.9 82.8 %all-gather.5.cloned.1.call-done = bf16[3072,1632]{1,0:T(8,128)(2,1)} async-done(((bf16[96,1632]{1,0:T(8,128)(2,1)}), bf16[3072,1632]{1,0:T(8,128)(2,1)}) %all-gather.5.cloned.1.call-update) | async-done | bytes 10027024 | tf_op jit(solution)/shard_map/all_gather | solution.py:136
  206.1 3.2 collective-permute-start
  213.9 7.7 collective-permute-done.1
  236.5 2.7 fusion.117
  241.8 2.6 fusion.119
  257.3 3.1 fusion.215
  285.9 3.1 collective-permute-start.2
  294.9 2.8 concatenate.246
  297.8 3.6 collective-permute-done.3
  319.6 2.8 fusion.110
  322.4 2.6 fusion.111
  327.6 2.6 fusion.113
  341.0 5.2 multiply_reduce_fusion.2
  346.2 2.9 fusion.10
  352.2 3.4 fusion.93
  357.4 4.3 fusion.160
  364.2 19.4 %fusion.29 = f32[12,64,320]{2,1,0:T(8,128)} fusion(bf16[192,12,64]{0,2,1:T(8,128)(2,1)} %get-tuple-element.181, f32[12,192,320]{2,1,0:T(8,128)} %fusion.217, f32[12,192,320]{2,1,0:T(8,128)} %copy-done, f32[12,192]{1,0:T(8,128)} %copy-done.78, pred[192,320]{1,0:T(8,128)(4,1)} %fusion.158), kind=kOutput, calls=%fused_computation.55 | convolution fusion | flops 102484544 | bytes 7246848 | tf_op jit(solution)/shard_map/hqk,qhd->khd/dot_general | solution.py:129
  392.3 3.1 collective-permute-start.4
  396.6 18.9 %fusion.57 = f32[192,12,64]{0,2,1:T(8,128)} fusion(bf16[320,12,64]{0,2,1:T(8,128)(2,1)} %bitcast.453, f32[12,192,320]{2,1,0:T(8,128)} %fusion.217, f32[12,192,320]{2,1,0:T(8,128)} %copy-done, f32[12,192]{1,0:T(8,128)} %copy-done.78, pred[192,320]{1,0:T(8,128)(4,1)} %fusion.158), kind=kOutput, calls=%fused_computation.76 | convolution fusion | flops 102484544 | bytes 7050240 | tf_op jit(solution)/shard_map/hqk,khd->qhd/dot_general | solution.py:126
  420.0 5.4 scatter-add.14
  425.4 2.7 fusion.131
  433.0 4.4 multiply_reduce_fusion.4
  448.8 2.9 fusion.11
  454.1 2.8 concatenate.261
  459.4 5.0 multiply_reduce_fusion.3
  464.4 2.9 fusion.12
  470.3 3.4 fusion.90
  475.6 3.3 fusion.163
  481.3 17.3 %fusion.35 = f32[12,64,320]{2,1,0:T(8,128)} fusion(bf16[192,12,64]{0,2,1:T(8,128)(2,1)} %get-tuple-element.183, f32[12,192,320]{2,1,0:T(8,128)} %fusion.218, f32[12,192,320]{2,1,0:T(8,128)S(1)} %get-tuple-element.192, f32[12,192]{1,0:T(8,128)S(1)} %log_add_fusion.1, pred[192,320]{1,0:T(8,128)(4,1)} %fusion.158), kind=kOutput, calls=%fused_computation.57 | convolution fusion | flops 102484544 | bytes 7246848 | tf_op jit(solution)/shard_map/hqk,qhd->khd/dot_general | solution.py:129
  498.6 3.0 fusion.22
  505.8 7.0 pad_maximum_fusion
  512.8 13.8 %copy.300 = bf16[4,768,1632]{2,1,0:T(8,128)(2,1)} copy(bf16[4,768,1632]{1,2,0:T(8,128)(2,1)} %pad_maximum_fusion) | data formatting | bytes 20054016 | tf_op jit(solution)/shard_map/concatenate | solution.py:369
  526.6 5.3 pad_maximum_fusion.1
  531.8 8.1 copy.301
  542.0 5.2 collective-permute-start.6
  548.7 16.8 %fusion.54 = f32[192,12,64]{0,2,1:T(8,128)} fusion(bf16[320,12,64]{0,2,1:T(8,128)(2,1)} %bitcast.449, f32[12,192,320]{2,1,0:T(8,128)} %fusion.218, f32[12,192,320]{2,1,0:T(8,128)S(1)} %get-tuple-element.192, f32[12,192]{1,0:T(8,128)S(1)} %log_add_fusion.1, pred[192,320]{1,0:T(8,128)(4,1)} %fusion.158), kind=kOutput, calls=%fused_computation.75 | convolution fusion | flops 102484544 | bytes 7050240 | tf_op jit(solution)/shard_map/hqk,khd->qhd/dot_general | solution.py:126
  565.5 2.8 collective-permute-done.7
  572.3 6.7 scatter-add.16
  585.4 6.7 copy.305
  593.3 257.8 %all-reduce.6.cloned.1.call-done = (bf16[8,4,96,1632]{3,2,0,1:T(8,128)(2,1)}, bf16[8,4,96,864]{3,2,0,1:T(8,128)(2,1)}, bf16[8,4,96,768]{3,2,0,1:T(8,128)(2,1)}) async-done(((bf16[8,4,96,1632]{3,2,0,1:T(8,128)(2,1)}, bf16[8,4,96,864]{3,2,0,1:T(8,128)(2,1)}, bf16[8,4,96,768]{3,2,0,1:T(8,128)(2,1)}), (bf16[8,4,96,1632]{3,2,0,1:T(8,128)(2,1)}, bf16[8,4,96,864]{3,2,0,1:T(8,128)(2,1)}, ...) | async-done | bytes 20054032
  856.8 3.3 concatenate.279
  860.3 4.2 multiply_reduce_fusion.5
  867.3 3.4 fusion.84
  871.7 2.9 collective-permute-done.10
  876.1 3.4 collective-permute-done.11
  882.1 3.8 collective-permute-done.12
  886.6 25.5 %reduce-scatter.7.cloned.1.call-done = bf16[1,96,3264]{2,1,0:T(8,128)(2,1)} async-done(((bf16[4,96,3264]{2,1,0:T(8,128)(2,1)}), bf16[1,96,3264]{2,1,0:T(8,128)(2,1)}) %reduce-scatter.7.cloned.1.call-update) | async-done | bytes 626704 | tf_op jit(solution)/shard_map/reduce_scatter | solution.py:385
  (449 shorter events, 220.5 us)
Async XLA Ops:
  7.2 9.0 copy-start.67
  7.2 99.6 %all-gather.7.cloned.1.call-start = ((), (), s32[]{:S(2)}) async-start(), calls=%async_computation.3 | async-start | bytes 10543104 | tf_op jit(solution)/shard_map/all_gather | solution.py:136
  9.3 7.4 copy-start.68
  18.9 174.8 %all-gather.5.cloned.1.call-start = ((), (), s32[]{:S(2)}) async-start(), calls=%async_computation.2 | async-start | bytes 10543104 | tf_op jit(solution)/shard_map/all_gather | solution.py:136
  22.1 829.0 %all-reduce.6.cloned.1.call-start = ((), (), s32[]{:S(2)}) async-start(), calls=%async_computation.4 | async-start | bytes 40894464
  22.2 188.7 %copy-start.13 = (bf16[192,768]{1,0:T(8,128)(2,1)}, bf16[192,768]{1,0:T(8,128)(2,1)S(1)}, u32[]{:S(2)}) copy-start(bf16[192,768]{1,0:T(8,128)(2,1)S(1)} %convert_element_type.180) | copy-start | bytes 884740
  22.5 179.3 %copy-start.38 = (f32[192,64]{0,1:T(8,128)}, f32[192,64]{0,1:T(8,128)S(1)}, u32[]{:S(2)}) copy-start(f32[192,64]{0,1:T(8,128)S(1)} %pad_maximum_fusion.34) | copy-start | bytes 147460
  22.8 182.1 %copy-start.31 = (f32[192,768]{1,0:T(8,128)}, f32[192,768]{1,0:T(8,128)S(1)}, u32[]{:S(2)}) copy-start(f32[192,768]{1,0:T(8,128)S(1)} %copy.251) | copy-start | bytes 1769476
  23.6 170.1 %copy-start.79 = (f32[768]{0:T(1024)}, f32[768]{0:T(1024)S(1)}, u32[]{:S(2)}) copy-start(f32[768]{0:T(1024)S(1)} %get-tuple-element.111) | copy-start | bytes 9220
  24.2 177.6 %copy-start.69 = (f32[192,64]{0,1:T(8,128)}, f32[192,64]{0,1:T(8,128)S(1)}, u32[]{:S(2)}) copy-start(f32[192,64]{0,1:T(8,128)S(1)} %pad_maximum_fusion.35) | copy-start | bytes 147460
  24.2 169.5 %copy-start.87 = (f32[192]{0:T(256)}, f32[192]{0:T(256)S(1)}, u32[]{:S(2)}) copy-start(f32[192]{0:T(256)S(1)} %broadcast_multiply_fusion.19) | copy-start | bytes 2308
  24.5 169.3 %copy-start.95 = (f32[192]{0:T(256)}, f32[192]{0:T(256)S(1)}, u32[]{:S(2)}) copy-start(f32[192]{0:T(256)S(1)} %add_rsqrt_fusion.3) | copy-start | bytes 2308
  25.4 173.8 %copy-start.34 = (bf16[192,768]{1,0:T(8,128)(2,1)}, bf16[192,768]{1,0:T(8,128)(2,1)S(1)}, u32[]{:S(2)}) copy-start(bf16[192,768]{1,0:T(8,128)(2,1)S(1)} %multiply_convert_fusion.15) | copy-start | bytes 884740
  206.1 7.8 collective-permute-start
  209.4 12.3 %collective-permute-start.1 = (bf16[64,1536]{1,0:T(8,128)(2,1)S(1)}, bf16[64,1536]{1,0:T(8,128)(2,1)S(1)}, u32[]{:S(2)}, u32[]{:S(2)}) collective-permute-start(bf16[64,1536]{1,0:T(8,128)(2,1)S(1)} %get-tuple-element.172), channel_id=1, source_target_pairs={{1,0},{2,1},{3,2},{4,3},{5,4},{6,5},{7,6},{8,7},{9,8},{10,9},{11,1... | collective-permute-start | bytes 589832 | tf_op jit(solution)/shard_map/ppermute | solution.py:31
  228.3 6.9 copy-start.6
  229.3 7.1 copy-start.75
  229.4 7.0 copy-start.81
  236.5 8.0 copy-start.24
  260.3 8.4 copy-start.21
  260.3 8.4 copy-start.91
  260.6 8.2 copy-start.99
  260.8 8.0 copy-start.36
  281.6 8.7 copy-start.14
  285.9 11.9 %collective-permute-start.2 = (bf16[64,1536]{1,0:T(8,128)(2,1)}, bf16[64,1536]{1,0:T(8,128)(2,1)}, u32[]{:S(2)}, u32[]{:S(2)}) collective-permute-start(bf16[64,1536]{1,0:T(8,128)(2,1)} %get-tuple-element.167), channel_id=1, source_target_pairs={{0,1},{1,2},{2,3},{3,4},{4,5},{5,6},{6,7},{7,8},{8,9},{9,10},{10,1... | collective-permute-start | bytes 589832 | tf_op jit(solution)/shard_map/ppermute | solution.py:29
  289.0 12.3 %collective-permute-start.3 = (bf16[64,1536]{1,0:T(8,128)(2,1)}, bf16[64,1536]{1,0:T(8,128)(2,1)}, u32[]{:S(2)}, u32[]{:S(2)}) collective-permute-start(bf16[64,1536]{1,0:T(8,128)(2,1)} %get-tuple-element.168), channel_id=1, source_target_pairs={{1,0},{2,1},{3,2},{4,3},{5,4},{6,5},{7,6},{8,7},{9,8},{10,9},{11,1... | collective-permute-start | bytes 589832 | tf_op jit(solution)/shard_map/ppermute | solution.py:31
  311.3 7.0 copy-start.22
  312.5 7.2 copy-start.76
  312.5 7.0 copy-start.85
  319.6 8.0 copy-start.26
  392.3 23.2 %collective-permute-start.4 = (bf16[64,1536]{0,1:T(8,128)(2,1)}, bf16[64,1536]{0,1:T(8,128)(2,1)}, u32[]{:S(2)}, u32[]{:S(2)}) collective-permute-start(bf16[64,1536]{0,1:T(8,128)(2,1)} %get-tuple-element.143), channel_id=1, source_target_pairs={{0,1},{1,2},{2,3},{3,4},{4,5},{5,6},{6,7},{7,8},{8,9},{9,10},{10,1... | collective-permute-start | bytes 589832 | tf_op jit(solution)/shard_map/ppermute | solution.py:29
  395.3 20.4 %collective-permute-start.5 = (bf16[64,1536]{0,1:T(8,128)(2,1)}, bf16[64,1536]{0,1:T(8,128)(2,1)}, u32[]{:S(2)}, u32[]{:S(2)}) collective-permute-start(bf16[64,1536]{0,1:T(8,128)(2,1)} %get-tuple-element.144), channel_id=1, source_target_pairs={{1,0},{2,1},{3,2},{4,3},{5,4},{6,5},{7,6},{8,7},{9,8},{10,9},{11,1... | collective-permute-start | bytes 589832 | tf_op jit(solution)/shard_map/ppermute | solution.py:31
  437.4 9.5 %copy-start.63 = (bf16[192,4,288]{0,2,1:T(8,128)(2,1)S(1)}, bf16[192,4,288]{0,2,1:T(8,128)(2,1)}, u32[]{:S(2)}) copy-start(bf16[192,4,288]{0,2,1:T(8,128)(2,1)} %copy-done.62) | copy-start | bytes 1327108
  438.5 10.3 %copy-start.37 = (bf16[192,768]{1,0:T(8,128)(2,1)S(1)}, bf16[192,768]{1,0:T(8,128)(2,1)}, u32[]{:S(2)}) copy-start(bf16[192,768]{1,0:T(8,128)(2,1)} %copy-done.36) | copy-start | bytes 884740
  498.6 7.2 copy-start.43
  542.0 23.5 %collective-permute-start.6 = (bf16[64,1536]{0,1:T(8,128)(2,1)}, bf16[64,1536]{0,1:T(8,128)(2,1)}, u32[]{:S(2)}, u32[]{:S(2)}) collective-permute-start(bf16[64,1536]{0,1:T(8,128)(2,1)} %get-tuple-element.141), channel_id=1, source_target_pairs={{0,1},{1,2},{2,3},{3,4},{4,5},{5,6},{6,7},{7,8},{8,9},{9,10},{10,1... | collective-permute-start | bytes 589832 | tf_op jit(solution)/shard_map/ppermute | solution.py:29
  547.2 21.1 %collective-permute-start.7 = (bf16[64,1536]{0,1:T(8,128)(2,1)}, bf16[64,1536]{0,1:T(8,128)(2,1)}, u32[]{:S(2)}, u32[]{:S(2)}) collective-permute-start(bf16[64,1536]{0,1:T(8,128)(2,1)} %get-tuple-element.142), channel_id=1, source_target_pairs={{1,0},{2,1},{3,2},{4,3},{5,4},{6,5},{7,6},{8,7},{9,8},{10,9},{11,1... | collective-permute-start | bytes 589832 | tf_op jit(solution)/shard_map/ppermute | solution.py:31
  565.5 6.8 copy-start.8
  572.3 7.1 copy-start.71
  592.1 319.9 %reduce-scatter.7.cloned.1.call-start = ((), (), s32[]{:S(2)}) async-start(), calls=%async_computation.1 | async-start | bytes 3194880 | tf_op jit(solution)/shard_map/reduce_scatter | solution.py:385
  860.3 7.1 copy-start.18
  860.3 7.1 copy-start.61
  864.5 16.6 %copy-start.64 = (f32[192,768]{1,0:T(8,128)S(1)}, f32[192,768]{1,0:T(8,128)}, u32[]{:S(2)}) copy-start(f32[192,768]{1,0:T(8,128)} %get-tuple-element.116) | copy-start | bytes 1769476
  864.5 1.2 collective-permute-start.8
  865.8 5.0 collective-permute-start.9
  870.8 3.8 collective-permute-start.10
  874.6 4.9 collective-permute-start.11
  879.5 6.5 collective-permute-start.12
  (78 other events, 249.8 us)
Sparse Core Ops, SparseCore 0:
  19.0 87.6 all-gather.6
  110.2 83.4 all-gather.4
  592.2 258.8 all-reduce.5
  860.3 51.7 reduce-scatter.6

commit v2 on v1

--- a/solution.py
+++ b/solution.py
@@ -3,6 +3,8 @@
 import jax
 import jax.numpy as jnp
 from jax import lax
+from jax.experimental import pallas as pl
+from jax.experimental.pallas import tpu as pltpu
 from jax.sharding import PartitionSpec as P
 
 D = 768
@@ -35,26 +37,14 @@
     return cells
 
 
-def rotate_half(values):
-    middle_state = values.shape[-1] // 2
-    return jnp.concatenate([-values[..., middle_state:], values[..., :middle_state]], axis=-1)
-
-
 def rope_tables(positions):
     middle_state = HDIM // 2
     inverse = THETA ** (-(jnp.arange(middle_state, dtype=jnp.float32) * (2.0 / HDIM)))
     angles = positions.astype(jnp.float32)[:, None] * inverse[None, :]
-    cosine = jnp.concatenate([jnp.cos(angles), jnp.cos(angles)], axis=1)
-    sine = jnp.concatenate([jnp.sin(angles), jnp.sin(angles)], axis=1)
-    return (cosine[:, None, :], sine[:, None, :])
-
-
-def apply_rope(values, cosine, sine):
-    return values * cosine + rotate_half(values) * sine
-
-
-def undo_rope(grads, cosine, sine):
-    return grads * cosine - rotate_half(grads * sine)
+    return (
+        jnp.concatenate([jnp.cos(angles)] * 4, axis=1),
+        jnp.concatenate([jnp.sin(angles)] * 4, axis=1),
+    )
 
 
 def layer_normalize(hidden_state):
@@ -85,51 +75,121 @@
     )
 
 
-def band_mask(query_pos, key_pos, length):
-    near = jnp.abs(query_pos[:, None] - key_pos[None, :]) <= WIN
-    same = query_pos[:, None] // length == key_pos[None, :] // length
-    return near & same
-
-
-def masked_scores(query_matrix, padded_keys, allowed):
-    scores = jnp.einsum(
-        "qhd,khd->hqk", query_matrix, padded_keys, preferred_element_type=jnp.float32
-    ) * (1.0 / math.sqrt(HDIM))
-    return jnp.where(allowed[None], scores, -1e30)
-
-
-def attend_forward(query_matrix, padded_keys, padded_values, allowed):
-    scores = masked_scores(query_matrix, padded_keys, allowed)
-    top = jnp.max(scores, axis=-1, keepdims=True)
-    log_total = top + jnp.log(jnp.sum(jnp.exp(scores - top), axis=-1, keepdims=True))
-    probs = jnp.exp(scores - log_total).astype(jnp.bfloat16)
-    context_rows = jnp.einsum(
-        "hqk,khd->qhd", probs, padded_values, preferred_element_type=jnp.float32
-    ).astype(jnp.bfloat16)
-    return (context_rows, log_total)
-
-
-def attend_backward(query_matrix, padded_keys, padded_values, allowed, log_total, grad_context):
-    scores = masked_scores(query_matrix, padded_keys, allowed)
-    probs = jnp.exp(scores - log_total)
-    grad_values = jnp.einsum(
-        "hqk,qhd->khd", probs.astype(jnp.bfloat16), grad_context, preferred_element_type=jnp.float32
-    )
-    grad_probs = jnp.einsum(
-        "qhd,khd->hqk", grad_context, padded_values, preferred_element_type=jnp.float32
-    )
-    grad_scores = (
-        probs
-        * (grad_probs - jnp.sum(probs * grad_probs, axis=-1, keepdims=True))
-        * (1.0 / math.sqrt(HDIM))
-    ).astype(jnp.bfloat16)
-    grad_queries = jnp.einsum(
-        "hqk,khd->qhd", grad_scores, padded_keys, preferred_element_type=jnp.float32
-    )
-    grad_keys = jnp.einsum(
-        "hqk,qhd->khd", grad_scores, query_matrix, preferred_element_type=jnp.float32
-    )
-    return (grad_queries, grad_keys, grad_values)
+def lane_half(shape):
+    return lax.rem(lax.broadcasted_iota(jnp.int32, shape, 1), HDIM) < HDIM // 2
+
+
+def rotate_lanes(values, sign):
+    width = values.shape[1]
+    ahead = pltpu.roll(values, width - HDIM // 2, 1)
+    behind = pltpu.roll(values, HDIM // 2, 1)
+    return jnp.where(lane_half(values.shape), -sign * ahead, sign * behind)
+
+
+def spread(table):
+    return jnp.concatenate([table] * (D // table.shape[1]), axis=1)
+
+
+def rope_kernel(qkv_ref, cosine_ref, sine_ref, query_ref, kv_ref):
+    cosine = spread(cosine_ref[...])
+    sine = spread(sine_ref[...])
+    queries = qkv_ref[:, :D]
+    keys = qkv_ref[:, D : 2 * D]
+    query_ref[...] = (queries * cosine + rotate_lanes(queries, 1.0) * sine).astype(jnp.bfloat16)
+    kv_ref[:, :D] = (keys * cosine + rotate_lanes(keys, 1.0) * sine).astype(jnp.bfloat16)
+    kv_ref[:, D:] = qkv_ref[:, 2 * D :].astype(jnp.bfloat16)
+
+
+def dot_f32(left, right, dims):
+    return lax.dot_general(left, right, (dims, ((), ())), preferred_element_type=jnp.float32)
+
+
+def head_scores(queries, keys, allowed):
+    scores = dot_f32(queries, keys, ((1,), (1,))) * (1.0 / math.sqrt(HDIM))
+    return jnp.where(allowed, scores, -1e30)
+
+
+def window_mask(bounds_ref, rows):
+    shape = (rows, rows + 2 * WIN)
+    query = lax.broadcasted_iota(jnp.int32, shape, 0)
+    key = lax.broadcasted_iota(jnp.int32, shape, 1)
+    near = (key >= query) & (key <= query + 2 * WIN)
+    return near & (key >= bounds_ref[0]) & (key < bounds_ref[1])
+
+
+def forward_kernel(bounds_ref, query_ref, kv_ref, context_ref, log_ref):
+    rows = query_ref.shape[0]
+    allowed = window_mask(bounds_ref, rows)
+    logs = []
+    for head in range(HEADS):
+        cols = slice(head * HDIM, (head + 1) * HDIM)
+        shifted = slice(D + head * HDIM, D + (head + 1) * HDIM)
+        scores = head_scores(query_ref[:, cols], kv_ref[:, cols], allowed)
+        top = jnp.max(scores, axis=1, keepdims=True)
+        log_total = top + jnp.log(jnp.sum(jnp.exp(scores - top), axis=1, keepdims=True))
+        probs = jnp.exp(scores - log_total).astype(jnp.bfloat16)
+        context_ref[:, cols] = dot_f32(probs, kv_ref[:, shifted], ((1,), (0,))).astype(
+            jnp.bfloat16
+        )
+        logs.append(log_total)
+    log_ref[...] = jnp.concatenate(logs, axis=1)
+
+
+def backward_kernel(
+    bounds_ref, query_ref, kv_ref, log_ref, grad_ref, dquery_ref, local_ref, rim_ref
+):
+    rows = query_ref.shape[0]
+    allowed = window_mask(bounds_ref, rows)
+    for head in range(HEADS):
+        cols = slice(head * HDIM, (head + 1) * HDIM)
+        shifted = slice(D + head * HDIM, D + (head + 1) * HDIM)
+        queries = query_ref[:, cols]
+        keys = kv_ref[:, cols]
+        grads = grad_ref[:, cols]
+        scores = head_scores(queries, keys, allowed)
+        probs = jnp.exp(scores - log_ref[:, head : head + 1])
+        grad_values = dot_f32(probs.astype(jnp.bfloat16), grads, ((0,), (0,)))
+        grad_probs = dot_f32(grads, kv_ref[:, shifted], ((1,), (1,)))
+        inner = jnp.sum(probs * grad_probs, axis=1, keepdims=True)
+        grad_scores = (probs * (grad_probs - inner) * (1.0 / math.sqrt(HDIM))).astype(jnp.bfloat16)
+        dquery_ref[:, cols] = dot_f32(grad_scores, keys, ((1,), (0,)))
+        grad_keys = dot_f32(grad_scores, queries, ((0,), (0,)))
+        for place, value in ((cols, grad_keys), (shifted, grad_values)):
+            local_ref[:, place] = value[WIN : WIN + rows]
+            rim_ref[:WIN, place] = value[:WIN].astype(jnp.bfloat16)
+            rim_ref[WIN:, place] = value[WIN + rows :].astype(jnp.bfloat16)
+
+
+def unrope_kernel(dquery_ref, local_ref, low_ref, high_ref, cosine_ref, sine_ref, out_ref):
+    rows = dquery_ref.shape[0]
+    cosine = spread(cosine_ref[...])
+    sine = spread(sine_ref[...])
+    queries = dquery_ref[...]
+    out_ref[:, :D] = (queries * cosine - rotate_lanes(queries * sine, 1.0)).astype(jnp.bfloat16)
+    local = local_ref[...]
+    top = jnp.concatenate([low_ref[...].astype(jnp.float32), jnp.zeros((rows - WIN, 2 * D), jnp.float32)], axis=0)
+    bottom = jnp.concatenate([jnp.zeros((rows - WIN, 2 * D), jnp.float32), high_ref[...].astype(jnp.float32)], axis=0)
+    local = local + top + bottom
+    keys = local[:, :D]
+    out_ref[:, D : 2 * D] = (keys * cosine - rotate_lanes(keys * sine, 1.0)).astype(jnp.bfloat16)
+    out_ref[:, 2 * D :] = local[:, D:].astype(jnp.bfloat16)
+
+
+def local_call(kernel, outs, flops, operands, scalars=False):
+    moved = sum(x.size * x.dtype.itemsize for x in operands) + sum(
+        math.prod(shape) * jnp.dtype(kind).itemsize for shape, kind in outs
+    )
+    specs = [pl.BlockSpec(memory_space=pltpu.VMEM)] * len(operands)
+    if scalars:
+        specs[0] = pl.BlockSpec(memory_space=pltpu.SMEM)
+    return pl.pallas_call(
+        kernel,
+        out_shape=[jax.ShapeDtypeStruct(shape, kind) for shape, kind in outs],
+        in_specs=specs,
+        out_specs=[pl.BlockSpec(memory_space=pltpu.VMEM)] * len(outs),
+        cost_estimate=pl.CostEstimate(flops=flops, bytes_accessed=moved, transcendentals=0),
+        compiler_params=pltpu.CompilerParams(vmem_limit_bytes=40 * 1024 * 1024),
+    )(*operands)
 
 
 def gather_all(share, n_w, n_seq):
@@ -140,7 +200,8 @@
 def sum_over_blocks(terms, n_w, n_seq):
     depth = terms.shape[1] // n_seq
     parts = terms.reshape(n_w, n_seq, depth, terms.shape[2]).transpose(1, 0, 2, 3)
-    return lax.psum_scatter(parts, "seq", scatter_dimension=0, tiled=True)[0]
+    parts = parts.reshape(n_seq * n_w, depth, terms.shape[2])
+    return lax.psum_scatter(parts, "seq", scatter_dimension=0, tiled=True)
 
 
 def sum_everywhere(values, axes):
@@ -172,8 +233,9 @@
     length = total_tokens // SEQS
     block_index = lax.axis_index("seq") * lax.axis_size("wshard") + lax.axis_index("wshard")
     query_pos = block_index * rows + jnp.arange(rows, dtype=jnp.int32)
-    key_pos = block_index * rows - WIN + jnp.arange(rows + 2 * WIN, dtype=jnp.int32)
-    allowed = band_mask(query_pos, key_pos, length)
+    begin = block_index * rows - WIN
+    first = begin + WIN - (begin + WIN) % length
+    bounds = jnp.stack([first - begin, first + length - begin]).astype(jnp.int32)
     cosine, sine = rope_tables(query_pos % length)
     scale_grad = 1.0 / math.sqrt(total_tokens)
     n_seq = lax.axis_size("seq")
@@ -244,22 +306,20 @@
             jnp.bfloat16
         )
         qkv = columns_product(attention_normalized, full_qkv)
-        query_matrix = apply_rope(qkv[:, :D].reshape(rows, HEADS, HDIM), cosine, sine).astype(
-            jnp.bfloat16
-        )
-        key_rows = (
-            apply_rope(qkv[:, D : 2 * D].reshape(rows, HEADS, HDIM), cosine, sine)
-            .astype(jnp.bfloat16)
-            .reshape(rows, D)
-        )
-        value_rows = qkv[:, 2 * D :].astype(jnp.bfloat16)
-        edged = with_halo(
-            jnp.concatenate([key_rows, value_rows], axis=1), ((("seq", "wshard"), 0),), WIN
-        )
-        padded_keys = edged[:, :D].reshape(rows + 2 * WIN, HEADS, HDIM)
-        padded_values = edged[:, D:].reshape(rows + 2 * WIN, HEADS, HDIM)
-        context_rows, log_total = attend_forward(query_matrix, padded_keys, padded_values, allowed)
-        context_rows = context_rows.reshape(rows, D)
+        query_matrix, kv_rows = local_call(
+            rope_kernel,
+            [((rows, D), jnp.bfloat16), ((rows, 2 * D), jnp.bfloat16)],
+            8 * rows * D,
+            (qkv, cosine, sine),
+        )
+        padded = with_halo(kv_rows, ((("seq", "wshard"), 0),), WIN)
+        context_rows, log_total = local_call(
+            forward_kernel,
+            [((rows, D), jnp.bfloat16), ((rows, HEADS), jnp.float32)],
+            4 * rows * padded.shape[0] * D,
+            (bounds, query_matrix, padded),
+            True,
+        )
         middle_state = hidden_state + columns_product(context_rows, full_out)
         feedforward_standardized, feedforward_inverse_deviation = layer_normalize(middle_state)
         feedforward_normalized = (
@@ -277,8 +337,7 @@
                 attention_inverse_deviation,
                 attention_normalized,
                 query_matrix,
-                padded_keys,
-                padded_values,
+                padded,
                 log_total,
                 context_rows,
                 feedforward_standardized,
@@ -298,8 +357,7 @@
             attention_inverse_deviation,
             attention_normalized,
             query_matrix,
-            padded_keys,
-            padded_values,
+            padded,
             log_total,
             context_rows,
             feedforward_standardized,
@@ -336,33 +394,29 @@
         grad_middle_rounded = grad_middle.astype(jnp.bfloat16)
         local_out = blocks(context_rows, grad_middle_rounded, col_out)
         grad_context = (
-            rows_product(grad_middle_rounded, full_out)
-            .astype(jnp.bfloat16)
-            .reshape(rows, HEADS, HDIM)
-        )
-        grad_queries, grad_keys, grad_values = attend_backward(
-            query_matrix, padded_keys, padded_values, allowed, log_total, grad_context
-        )
-        edge_terms = jnp.concatenate(
-            [grad_keys.reshape(rows + 2 * WIN, D), grad_values.reshape(rows + 2 * WIN, D)], axis=1
-        )
-        rims = jnp.concatenate([edge_terms[:WIN], edge_terms[rows + WIN :]], axis=0)
-        returned = with_halo(rims.astype(jnp.bfloat16), ((("seq", "wshard"), 0),), WIN).astype(
-            rims.dtype
-        )
-        local_terms = edge_terms[WIN : WIN + rows]
-        local_terms = (
-            local_terms.at[:WIN].add(returned[:WIN]).at[rows - WIN :].add(returned[3 * WIN :])
-        )
-        grad_keys_local = local_terms[:, :D].reshape(rows, HEADS, HDIM)
-        grad_qkv = jnp.concatenate(
+            rows_product(grad_middle_rounded, full_out).astype(jnp.bfloat16)
+        )
+        grad_queries, local_terms, rims = local_call(
+            backward_kernel,
             [
-                undo_rope(grad_queries, cosine, sine).reshape(rows, D),
-                undo_rope(grad_keys_local, cosine, sine).reshape(rows, D),
-                local_terms[:, D:],
+                ((rows, D), jnp.float32),
+                ((rows, 2 * D), jnp.float32),
+                ((2 * WIN, 2 * D), jnp.bfloat16),
             ],
-            axis=1,
-        ).astype(jnp.bfloat16)
+            10 * rows * padded.shape[0] * D,
+            (bounds, query_matrix, padded, log_total, grad_context),
+            True,
+        )
+        sites = ("seq", "wshard")
+        count = lax.axis_size(sites)
+        low = lax.ppermute(rims[WIN:], sites, [(i, i + 1) for i in range(count - 1)])
+        high = lax.ppermute(rims[:WIN], sites, [(i + 1, i) for i in range(count - 1)])
+        (grad_qkv,) = local_call(
+            unrope_kernel,
+            [((rows, 3 * D), jnp.bfloat16)],
+            12 * rows * D,
+            (grad_queries, local_terms, low, high, cosine, sine),
+        )
         local_qkv = blocks(attention_normalized, grad_qkv, col_qkv)
         block_sums.append(
             sum_over_blocks(

time: 933 us -> 681 us (0.73)
  waiting for transfers between devices: 474 us -> 363 us
  matrix products: 205 us -> 105 us
  local copies, waits for them, and re-layouts: 132 us -> 98.5 us
  other arithmetic: 70.9 us -> 40 us
  Pallas kernels: 0 us -> 28.6 us
    unnamed x5 -> x6, waiting for transfers between devices: 258 us -> 0.1 us
    reduce_scatter x0 -> x3, waiting for transfers between devices: none -> 129 us  [sum_over_blocks(): return lax.psum_scatter(parts, 'seq', scatter_dimension=0, tiled=True)]
    dot_general x12 -> x0, matrix products: 91.3 us -> none  [the longest x2 36.6 us: attend_backward(): jnp.einsum('hqk,qhd->khd', grad_scores, query_matrix, preferred_element_t...]
    pallas_call x0 -> x8, Pallas kernels: none -> 28.6 us  [local_call(): pl.pallas_call(kernel, out_shape=[jax.ShapeDtypeStruct(shape, kind) for s...]
    transpose x0 -> x3, local copies, waits for them, and re-layouts: none -> 21 us  [sum_over_blocks(): terms.reshape(n_w, n_seq, depth, terms.shape[2]).transpose(1, 0, 2, 3)]
    ppermute x0 -> x4, waiting for transfers between devices: none -> 20.4 us  [the longest x2 17.6 us: per_device(): lax.ppermute(rims[:WIN], sites, [(i + 1, i) for i in range(count - 1)])]
    slice x16 -> x4, local copies, waits for them, and re-layouts: 17.8 us -> 0.79 us  [the longest x2 0.73 us: with_halo(): head = lax.slice_in_dim(cells, 0, width, axis=dim)]
    scatter-add x2 -> x0, local copies, waits for them, and re-layouts: 12 us -> none  [per_device(): local_terms.at[:WIN].add(returned[:WIN]).at[rows - WIN:]]
  transfers between devices with their start and end apart: 17 -> 19, of which waited for: 13 -> 16; matrix products, arithmetic and copies ran while one was open for 7% -> 15% of each run, Pallas kernels for 0% -> 0%
where the time goes in v2:
time: 681 us; the launch traced here: 673 us
  waiting for transfers between devices  363 us (53%)
  matrix products  105 us (15%)
  local copies, waits for them, and re-layouts  98.5 us (14%)
  other arithmetic  40 us (6%)
  Pallas kernels  28.6 us (4%)
  starting transfers between devices  22.2 us (3%)
  between operations  15.8 us (2%)
    all_gather x2, waiting for transfers between devices, gather_all(): whole = lax.all_gather(share, ('wshard', 'seq'), axis=0, tiled=False)  161 us
    reduce_scatter x3, waiting for transfers between devices, sum_over_blocks(): return lax.psum_scatter(parts, 'seq', scatter_dimension=0, tiled=True)  129 us
    dot_general x32, matrix products, columns_product(): jnp.dot(left, weight[i], preferred_element_type=jnp.float32)  63.5 us
    dot_general x8, matrix products, rows_product(): jnp.einsum('twf,wdf->td', left.reshape(rows, n_w, weight.shape[2]), weigh...  30.6 us
    pallas_call x8, Pallas kernels, local_call(): pl.pallas_call(kernel, out_shape=[jax.ShapeDtypeStruct(shape, kind) for s...  28.6 us
    reduce_scatter x1, waiting for transfers between devices, per_device(): lax.psum_scatter(jnp.concatenate(block_sums, axis=2), 'wshard', scatter_d...  25.5 us
    concatenate x14, local copies, waits for them, and re-layouts, columns_product(): jnp.concatenate([jnp.dot(left, weight[i], preferred_element_type=jnp.floa...  22.2 us
    transpose x3, local copies, waits for them, and re-layouts, sum_over_blocks(): terms.reshape(n_w, n_seq, depth, terms.shape[2]).transpose(1, 0, 2, 3)  21 us
  transfers between devices with their start and end apart: 19, of which 16 were waited for; matrix products, arithmetic and copies ran while one was open for 15% of the time, Pallas kernels for 0%

profile of v2, /device:TPU:0, one launch (start us, length us, event | category | flops | bytes accessed | tf_op | source)
XLA Modules:
  0.0 673.1 jit_solution(474436182724819620)
XLA Ops:
  7.2 2.6 fusion.126
  19.3 84.2 %all-gather.5.cloned.1.call-done = bf16[3072,1632]{1,0:T(8,128)(2,1)} async-done(((bf16[96,1632]{1,0:T(8,128)(2,1)}), bf16[3072,1632]{1,0:T(8,128)(2,1)}) %all-gather.5.cloned.1.call-update) | async-done | bytes 10027024 | tf_op jit(solution)/shard_map/all_gather | solution.py:196
  108.3 2.4 fusion.87
  113.1 76.9 %all-gather.7.cloned.1.call-done = bf16[3072,1632]{1,0:T(8,128)(2,1)} async-done(((bf16[96,1632]{1,0:T(8,128)(2,1)}), bf16[3072,1632]{1,0:T(8,128)(2,1)}) %all-gather.7.cloned.1.call-update) | async-done | bytes 10027024 | tf_op jit(solution)/shard_map/all_gather | solution.py:196
  196.9 3.2 collective-permute-start
  204.8 7.7 %collective-permute-done.1 = bf16[64,1536]{1,0:T(8,128)(2,1)S(1)} collective-permute-done((bf16[64,1536]{1,0:T(8,128)(2,1)S(1)}, bf16[64,1536]{1,0:T(8,128)(2,1)S(1)}, u32[]{:S(2)}, u32[]{:S(2)}) %collective-permute-start.1) | collective-permute-done | bytes 196640 | tf_op jit(solution)/shard_map/ppermute | solution.py:33
  212.5 5.8 shard_map.144
  226.4 2.8 fusion.83
  229.1 2.6 fusion.84
  231.8 2.6 fusion.85
  242.6 2.9 fusion.134
  246.0 2.5 fusion.81
  248.5 2.4 fusion.80
  253.3 2.4 fusion.78
  259.2 2.5 collective-permute-start.2
  268.2 6.6 collective-permute-done.3
  274.9 5.8 shard_map.146
  297.0 5.3 multiply_reduce_fusion
  304.6 2.7 fusion.57.grad_ref
  307.3 6.6 shard_map.147
  319.8 9.3 %collective-permute-done.5.high_ref = bf16[64,1536]{1,0:T(8,128)(2,1)S(1)} collective-permute-done((bf16[64,1536]{1,0:T(8,128)(2,1)S(1)}, bf16[64,1536]{1,0:T(8,128)(2,1)S(1)}, u32[]{:S(2)}, u32[]{:S(2)}) %collective-permute-start.5) | collective-permute-done | bytes 196640 | tf_op jit(solution)/shard_map/ppermute | solution.py:413
  332.1 4.7 multiply_reduce_fusion.2
  347.0 2.4 concatenate.160
  349.4 2.8 concatenate.161
  354.4 4.9 multiply_reduce_fusion.1
  361.3 2.6 fusion.54.grad_ref
  364.0 6.9 %shard_map.149 = (f32[192,768]{1,0:T(8,128)S(1)}, f32[192,1536]{1,0:T(8,128)S(1)}, bf16[128,1536]{1,0:T(8,128)(2,1)S(1)}) custom-call(s32[2]{0:T(128)S(1)} %pad_add_fusion.bounds_ref, bf16[192,768]{1,0:T(8,128)(2,1)S(1)} %get-tuple-element.22.query_ref, bf16[320,1536]{1,0:T(8,128)(2,1)S(1)} %copy-done.1, f32[192,12]{1,0:T(8,128)S(1)} %get-tuple-element.32.log_ref, ...), custom_call_target="tpu_custom_call" | custom-call | flops 471859200 | bytes 3744776 | tf_op jit(solution)/shard_map/pallas_call | solution.py:185
  374.6 2.5 fusion.23
  377.7 8.3 %collective-permute-done.7.high_ref = bf16[64,1536]{1,0:T(8,128)(2,1)S(1)} collective-permute-done((bf16[64,1536]{1,0:T(8,128)(2,1)S(1)}, bf16[64,1536]{1,0:T(8,128)(2,1)S(1)}, u32[]{:S(2)}, u32[]{:S(2)}) %collective-permute-start.7) | collective-permute-done | bytes 196640 | tf_op jit(solution)/shard_map/ppermute | solution.py:413
  389.1 2.4 fusion.11
  391.5 3.8 pad_maximum_fusion.2
  395.2 6.6 copy.118
  401.9 4.9 copy.119
  408.7 2.7 pad_maximum_fusion.1
  411.5 8.4 %copy.114 = bf16[4,768,864]{2,1,0:T(8,128)(2,1)} copy(bf16[4,768,864]{1,2,0:T(8,128)(2,1)} %pad_maximum_fusion.1) | data formatting | bytes 10616832 | tf_op jit(solution)/shard_map/concatenate | solution.py:382
  419.9 5.7 copy.115
  435.9 14.4 %pad_maximum_fusion = bf16[4,768,1632]{1,2,0:T(8,128)(2,1)} fusion(bf16[4,768,192]{1,2,0:T(8,128)(2,1)S(1)} %fusion.22, bf16[4,768,576]{1,2,0:T(8,128)(2,1)S(1)} %fusion.9, bf16[4,768,288]{1,2,0:T(8,128)(2,1)S(1)} %fusion.20, bf16[4,768,576]{1,2,0:T(8,128)(2,1)S(1)} %fusion.8), kind=kLoop, calls=%fused_computation | loop fusion | flops 40108032 | bytes 20054016 | tf_op jit(solution)/shard_map/concatenate | solution.py:423
  450.2 14.1 %copy.112 = bf16[4,768,1632]{2,1,0:T(8,128)(2,1)} copy(bf16[4,768,1632]{1,2,0:T(8,128)(2,1)} %pad_maximum_fusion) | data formatting | bytes 20054016 | tf_op jit(solution)/shard_map/concatenate | solution.py:423
  464.3 10.3 %copy.113 = bf16[8,4,96,1632]{3,2,1,0:T(8,128)(2,1)} copy(bf16[8,4,96,1632]{3,2,0,1:T(8,128)(2,1)} %bitcast.276) | data formatting | bytes 20054016 | tf_op jit(solution)/shard_map/transpose | solution.py:202
  474.8 44.9 %reduce-scatter.7.cloned.1.call-done = bf16[4,96,864]{2,1,0:T(8,128)(2,1)} async-done(((bf16[32,96,864]{2,1,0:T(8,128)(2,1)}), bf16[4,96,864]{2,1,0:T(8,128)(2,1)}) %reduce-scatter.7.cloned.1.call-update) | async-done | bytes 663568 | tf_op jit(solution)/shard_map/reduce_scatter | solution.py:204
  519.7 84.0 %reduce-scatter.5.cloned.1.call-done = bf16[4,96,1632]{2,1,0:T(8,128)(2,1)} async-done(((bf16[32,96,1632]{2,1,0:T(8,128)(2,1)}), bf16[4,96,1632]{2,1,0:T(8,128)(2,1)}) %reduce-scatter.5.cloned.1.call-update) | async-done | bytes 1253392 | tf_op jit(solution)/shard_map/reduce_scatter | solution.py:204
  603.7 5.6 concatenate.173
  609.5 4.0 multiply_reduce_fusion.3
  616.4 3.4 fusion.48
  620.7 2.9 collective-permute-done.10
  625.1 3.5 collective-permute-done.11
  631.2 3.9 collective-permute-done.12
  635.7 25.5 %reduce-scatter.11.cloned.1.call-done = bf16[1,96,3264]{2,1,0:T(8,128)(2,1)} async-done(((bf16[4,96,3264]{2,1,0:T(8,128)(2,1)}), bf16[1,96,3264]{2,1,0:T(8,128)(2,1)}) %reduce-scatter.11.cloned.1.call-update) | async-done | bytes 626704 | tf_op jit(solution)/shard_map/reduce_scatter | solution.py:439
  (303 shorter events, 131.3 us)
Async XLA Ops:
  7.2 96.3 %all-gather.5.cloned.1.call-start = ((), (), s32[]{:S(2)}) async-start(), calls=%async_computation.8 | async-start | bytes 10543104 | tf_op jit(solution)/shard_map/all_gather | solution.py:196
  15.7 174.3 %all-gather.7.cloned.1.call-start = ((), (), s32[]{:S(2)}) async-start(), calls=%async_computation.9 | async-start | bytes 10543104 | tf_op jit(solution)/shard_map/all_gather | solution.py:196
  17.2 457.6 %reduce-scatter.9.cloned.1.call-start = ((), (), s32[]{:S(2)}) async-start(), calls=%async_computation.6 | async-start | bytes 5308416 | tf_op jit(solution)/shard_map/reduce_scatter | solution.py:204
  17.3 184.4 %copy-start.4 = (bf16[192,768]{1,0:T(8,128)(2,1)}, bf16[192,768]{1,0:T(8,128)(2,1)S(1)}, u32[]{:S(2)}) copy-start(bf16[192,768]{1,0:T(8,128)(2,1)S(1)} %convert_element_type.110) | copy-start | bytes 884740
  18.9 177.2 %copy-start.48 = (f32[192]{0:T(256)}, f32[192]{0:T(256)S(1)}, u32[]{:S(2)}) copy-start(f32[192]{0:T(256)S(1)} %broadcast_multiply_fusion.15) | copy-start | bytes 2308
  19.1 177.8 %copy-start.54 = (f32[192]{0:T(256)}, f32[192]{0:T(256)S(1)}, u32[]{:S(2)}) copy-start(f32[192]{0:T(256)S(1)} %add_rsqrt_fusion.3) | copy-start | bytes 2308
  19.3 176.8 %copy-start.10 = (bf16[192,768]{1,0:T(8,128)(2,1)}, bf16[192,768]{1,0:T(8,128)(2,1)S(1)}, u32[]{:S(2)}) copy-start(bf16[192,768]{1,0:T(8,128)(2,1)S(1)} %multiply_convert_fusion.13) | copy-start | bytes 884740
  196.9 7.8 %collective-permute-start = (bf16[64,1536]{1,0:T(8,128)(2,1)S(1)}, bf16[64,1536]{1,0:T(8,128)(2,1)S(1)}, u32[]{:S(2)}, u32[]{:S(2)}) collective-permute-start(bf16[64,1536]{1,0:T(8,128)(2,1)S(1)} %get-tuple-element.109), channel_id=1, source_target_pairs={{0,1},{1,2},{2,3},{3,4},{4,5},{5,6},{6,7},{7,8},{8,9},{9,10},{10,1... | collective-permute-start | bytes 589832 | tf_op jit(solution)/shard_map/ppermute | solution.py:31
  200.2 12.3 %collective-permute-start.1 = (bf16[64,1536]{1,0:T(8,128)(2,1)S(1)}, bf16[64,1536]{1,0:T(8,128)(2,1)S(1)}, u32[]{:S(2)}, u32[]{:S(2)}) collective-permute-start(bf16[64,1536]{1,0:T(8,128)(2,1)S(1)} %get-tuple-element.108), channel_id=1, source_target_pairs={{1,0},{2,1},{3,2},{4,3},{5,4},{6,5},{7,6},{8,7},{9,8},{10,9},{11,1... | collective-permute-start | bytes 589832 | tf_op jit(solution)/shard_map/ppermute | solution.py:33
  212.5 21.9 %copy-start = (bf16[320,1536]{1,0:T(8,128)(2,1)}, bf16[320,1536]{1,0:T(8,128)(2,1)S(1)}, u32[]{:S(2)}) copy-start(bf16[320,1536]{1,0:T(8,128)(2,1)S(1)} %constant_dynamic-update-slice_fusion.kv_ref) | copy-start | bytes 2949124
  224.0 18.6 %copy-start.6 = (f32[192,768]{1,0:T(8,128)}, f32[192,768]{1,0:T(8,128)S(1)}, u32[]{:S(2)}) copy-start(f32[192,768]{1,0:T(8,128)S(1)} %get-tuple-element.85) | copy-start | bytes 1769476
  224.0 18.6 %copy-start.50 = (f32[192]{0:T(256)}, f32[192]{0:T(256)S(1)}, u32[]{:S(2)}) copy-start(f32[192]{0:T(256)S(1)} %broadcast_multiply_fusion.14) | copy-start | bytes 2308
  224.2 18.4 %copy-start.56 = (f32[192]{0:T(256)}, f32[192]{0:T(256)S(1)}, u32[]{:S(2)}) copy-start(f32[192]{0:T(256)S(1)} %add_rsqrt_fusion.2) | copy-start | bytes 2308
  224.4 18.2 %copy-start.13 = (bf16[192,768]{1,0:T(8,128)(2,1)}, bf16[192,768]{1,0:T(8,128)(2,1)S(1)}, u32[]{:S(2)}) copy-start(bf16[192,768]{1,0:T(8,128)(2,1)S(1)} %multiply_convert_fusion.12) | copy-start | bytes 884740
  226.3 14.5 %copy-start.24 = (f32[192,576]{1,0:T(8,128)}, f32[192,576]{1,0:T(8,128)S(1)}, u32[]{:S(2)}) copy-start(f32[192,576]{1,0:T(8,128)S(1)} %fusion.82) | copy-start | bytes 1327108
  242.6 10.7 %copy-start.30 = (bf16[192,4,288]{0,2,1:T(8,128)(2,1)}, bf16[192,4,288]{0,2,1:T(8,128)(2,1)S(1)}, u32[]{:S(2)}) copy-start(bf16[192,4,288]{0,2,1:T(8,128)(2,1)S(1)} %fusion.60) | copy-start | bytes 1327108
  259.2 9.0 %collective-permute-start.2 = (bf16[64,1536]{1,0:T(8,128)(2,1)}, bf16[64,1536]{1,0:T(8,128)(2,1)S(1)}, u32[]{:S(2)}, u32[]{:S(2)}) collective-permute-start(bf16[64,1536]{1,0:T(8,128)(2,1)} %get-tuple-element.105), channel_id=1, source_target_pairs={{0,1},{1,2},{2,3},{3,4},{4,5},{5,6},{6,7},{7,8},{8,9},{9,10},{10,1... | collective-permute-start | bytes 589832 | tf_op jit(solution)/shard_map/ppermute | solution.py:31
  266.3 19.8 %copy-start.9 = (f32[192,768]{1,0:T(8,128)S(1)}, f32[192,768]{1,0:T(8,128)}, u32[]{:S(2)}) copy-start(f32[192,768]{1,0:T(8,128)} %copy-done.8) | copy-start | bytes 1769476
  266.3 8.6 %collective-permute-start.3 = (bf16[64,1536]{1,0:T(8,128)(2,1)S(1)}, bf16[64,1536]{1,0:T(8,128)(2,1)S(1)}, u32[]{:S(2)}, u32[]{:S(2)}) collective-permute-start(bf16[64,1536]{1,0:T(8,128)(2,1)S(1)} %get-tuple-element.104), channel_id=1, source_target_pairs={{1,0},{2,1},{3,2},{4,3},{5,4},{6,5},{7,6},{8,7},{9,8},{10,9},{11,1... | collective-permute-start | bytes 589832 | tf_op jit(solution)/shard_map/ppermute | solution.py:33
  280.7 15.7 %copy-start.27 = (f32[192,2,576]{2,1,0:T(2,128)S(1)}, f32[192,2,576]{2,1,0:T(2,128)}, u32[]{:S(2)}) copy-start(f32[192,2,576]{2,1,0:T(2,128)} %concatenate.152) | copy-start | bytes 2654212
  286.2 10.9 %copy-start.47 = (f32[768]{0:T(1024)S(1)}, f32[768]{0:T(1024)}, u32[]{:S(2)}) copy-start(f32[768]{0:T(1024)} %get-tuple-element.72) | copy-start | bytes 9220
  287.6 14.8 %copy-start.15 = (bf16[192,768]{1,0:T(8,128)(2,1)}, bf16[192,768]{1,0:T(8,128)(2,1)S(1)}, u32[]{:S(2)}) copy-start(bf16[192,768]{1,0:T(8,128)(2,1)S(1)} %multiply_convert_fusion.10) | copy-start | bytes 884740
  304.6 32.3 %copy-start.36 = (bf16[192,768]{0,1:T(8,128)(2,1)}, bf16[192,768]{0,1:T(8,128)(2,1)S(1)}, u32[]{:S(2)}) copy-start(bf16[192,768]{0,1:T(8,128)(2,1)S(1)} %copy.151) | copy-start | bytes 884740
  313.9 23.0 %copy-start.53 = (f32[192]{0:T(256)S(1)}, f32[192]{0:T(256)}, u32[]{:S(2)}) copy-start(f32[192]{0:T(256)} %copy-done.52) | copy-start | bytes 2308
  313.9 23.0 %copy-start.59 = (f32[192]{0:T(256)S(1)}, f32[192]{0:T(256)}, u32[]{:S(2)}) copy-start(f32[192]{0:T(256)} %copy-done.58) | copy-start | bytes 2308
  314.0 5.8 collective-permute-start.4
  316.3 12.7 %collective-permute-start.5 = (bf16[64,1536]{1,0:T(8,128)(2,1)S(1)}, bf16[64,1536]{1,0:T(8,128)(2,1)S(1)}, u32[]{:S(2)}, u32[]{:S(2)}) collective-permute-start(bf16[64,1536]{1,0:T(8,128)(2,1)S(1)} %get-tuple-element.112), channel_id=1, source_target_pairs={{1,0},{2,1},{3,2},{4,3},{5,4},{6,5},{7,6},{8,7},{9,8},{10,9},{11,1... | collective-permute-start | bytes 589832 | tf_op jit(solution)/shard_map/ppermute | solution.py:413
  336.9 15.4 %copy-start.25 = (f32[192,576]{1,0:T(8,128)S(1)}, f32[192,576]{1,0:T(8,128)}, u32[]{:S(2)}) copy-start(f32[192,576]{1,0:T(8,128)} %copy-done.24) | copy-start | bytes 1327108
  336.9 15.4 %copy-start.26 = (f32[192,576]{1,0:T(8,128)S(1)}, f32[192,576]{1,0:T(8,128)}, u32[]{:S(2)}) copy-start(f32[192,576]{1,0:T(8,128)} %fusion.83) | copy-start | bytes 1327108
  336.9 17.5 %copy-start.51 = (f32[192]{0:T(256)S(1)}, f32[192]{0:T(256)}, u32[]{:S(2)}) copy-start(f32[192]{0:T(256)} %copy-done.50) | copy-start | bytes 2308
  336.9 17.5 %copy-start.57 = (f32[192]{0:T(256)S(1)}, f32[192]{0:T(256)}, u32[]{:S(2)}) copy-start(f32[192]{0:T(256)} %copy-done.56) | copy-start | bytes 2308
  370.9 6.8 %collective-permute-start.6 = (bf16[64,1536]{1,0:T(8,128)(2,1)S(1)}, bf16[64,1536]{1,0:T(8,128)(2,1)S(1)}, u32[]{:S(2)}, u32[]{:S(2)}) collective-permute-start(bf16[64,1536]{1,0:T(8,128)(2,1)S(1)} %get-tuple-element.111), channel_id=1, source_target_pairs={{0,1},{1,2},{2,3},{3,4},{4,5},{5,6},{6,7},{7,8},{8,9},{9,10},{10,1... | collective-permute-start | bytes 589832 | tf_op jit(solution)/shard_map/ppermute | solution.py:412
  373.3 12.7 %collective-permute-start.7 = (bf16[64,1536]{1,0:T(8,128)(2,1)S(1)}, bf16[64,1536]{1,0:T(8,128)(2,1)S(1)}, u32[]{:S(2)}, u32[]{:S(2)}) collective-permute-start(bf16[64,1536]{1,0:T(8,128)(2,1)S(1)} %get-tuple-element.110), channel_id=1, source_target_pairs={{1,0},{2,1},{3,2},{4,3},{5,4},{6,5},{7,6},{8,7},{9,8},{10,9},{11,1... | collective-permute-start | bytes 589832 | tf_op jit(solution)/shard_map/ppermute | solution.py:413
  406.9 112.8 %reduce-scatter.7.cloned.1.call-start = ((), (), s32[]{:S(2)}) async-start(), calls=%async_computation.5 | async-start | bytes 6193152 | tf_op jit(solution)/shard_map/reduce_scatter | solution.py:204
  425.6 178.2 %reduce-scatter.5.cloned.1.call-start = ((), (), s32[]{:S(2)}) async-start(), calls=%async_computation.4 | async-start | bytes 11501568 | tf_op jit(solution)/shard_map/reduce_scatter | solution.py:204
  474.7 134.7 %copy-start.62 = (f32[768]{0:T(1024)S(1)}, f32[768]{0:T(1024)}, u32[]{:S(2)}) copy-start(f32[768]{0:T(1024)} %get-tuple-element.66) | copy-start | bytes 9220
  474.7 134.8 %copy-start.63 = (f32[768]{0:T(1024)S(1)}, f32[768]{0:T(1024)}, u32[]{:S(2)}) copy-start(f32[768]{0:T(1024)} %get-tuple-element.62) | copy-start | bytes 9220
  474.7 134.8 %copy-start.3 = (f32[192,768]{1,0:T(8,128)S(1)}, f32[192,768]{1,0:T(8,128)}, u32[]{:S(2)}) copy-start(f32[192,768]{1,0:T(8,128)} %param.8) | copy-start | bytes 1769476
  474.7 134.8 %copy-start.49 = (f32[192]{0:T(256)S(1)}, f32[192]{0:T(256)}, u32[]{:S(2)}) copy-start(f32[192]{0:T(256)} %copy-done.48) | copy-start | bytes 2308
  474.7 134.8 %copy-start.55 = (f32[192]{0:T(256)S(1)}, f32[192]{0:T(256)}, u32[]{:S(2)}) copy-start(f32[192]{0:T(256)} %copy-done.54) | copy-start | bytes 2308
  474.7 141.7 %copy-start.34 = (bf16[192,4,288]{0,2,1:T(8,128)(2,1)S(1)}, bf16[192,4,288]{0,2,1:T(8,128)(2,1)}, u32[]{:S(2)}) copy-start(bf16[192,4,288]{0,2,1:T(8,128)(2,1)} %copy-done.33) | copy-start | bytes 1327108
  474.7 186.5 %reduce-scatter.11.cloned.1.call-start = ((), (), s32[]{:S(2)}) async-start(), calls=%async_computation.7 | async-start | bytes 3194880 | tf_op jit(solution)/shard_map/reduce_scatter | solution.py:439
  609.4 20.8 %copy-start.32 = (f32[192,768]{1,0:T(8,128)S(1)}, f32[192,768]{1,0:T(8,128)}, u32[]{:S(2)}) copy-start(f32[192,768]{1,0:T(8,128)} %get-tuple-element.77) | copy-start | bytes 1769476
  613.6 1.2 collective-permute-start.8
  614.8 5.0 collective-permute-start.9
  619.9 3.8 collective-permute-start.10
  623.6 5.0 collective-permute-start.11
  628.6 6.5 collective-permute-start.12
  (35 other events, 228.7 us)
Sparse Core Ops, SparseCore 0:
  15.8 87.6 all-gather.4
  106.4 83.4 all-gather.6
  407.0 51.5 reduce-scatter.8
  461.9 57.7 reduce-scatter.6
  523.2 80.5 reduce-scatter.4
  609.5 51.6 reduce-scatter.10
